TPU v7x, 256 devices: a whole 4x4x8 slice. The times are simulated.
256 devices in a mesh: cuts: 2 (over core), tile: 128 (over z, x, y).
Axes of the slice: x: 4, y: 4, z: 8, core: 2. Of those that a mesh axis runs over, the one named last changes fastest.
Arguments:
- object_slices: float32 [2, 2, 2048, 32768], P('cuts', None, None, 'tile'), may hold values from -5 to 5
- probe_field: float32 [2, 256, 256], replicated, may hold values from -4 to 4
- slice_phase: float32 [2, 256, 256], P('cuts'), may hold values from -3.140625 to 3.140625
- intensity: float32 [128, 8, 256, 256], P('tile'), may hold values from 0 to 1
- counts: int32 [128], P('tile'), may hold values from 1 to 6, as said below
- chosen: int32 [128, 6], P('tile'), may hold values from 0 to 7, as said below
- row_offset: int32 [128, 8], P('tile'), may hold values from 0 to 1792
- column_offset: int32 [128, 8], P('tile'), may hold values from 0 to 255
Outputs:
- object_grad: float32 [2, 2, 2048, 32768], P('cuts', None, None, 'tile')
Inputs may be any that keep to these rules, and one draw needn't show every extreme that they name: `counts`: live slots of a tile; some tile has exactly 6. `chosen`: distinct within a tile.
All inputs are finite; a program needn't handle non-finite values.
Results may differ from a plain program's by a relative error of at most 0.039.
Values may be sent and summed in bfloat16 or wider, within the bound.
A program may use at most 128 MiB of HBM per device.

v0:
```python
import jax
import jax.numpy as jnp
from jax import lax
from jax.sharding import PartitionSpec as P


def from_behind(value, axis, steps):
    count = lax.axis_size(axis)
    first, last = (max(0, -steps), min(count, count - steps))
    return lax.ppermute(value, axis, [(source, source + steps) for source in range(first, last)])


def make_table(length, direction):
    index = jnp.arange(length, dtype=jnp.int32)
    product = index[:, None] * index[None, :] % length
    angle = product.astype(jnp.float32) * (2.0 * jnp.pi / length)
    scale = length ** (-0.5)
    cosine = jnp.cos(angle) * scale
    sine = direction * jnp.sin(angle) * scale
    matrix = jnp.stack([jnp.stack([cosine, sine]), jnp.stack([-sine, cosine])])
    return matrix.astype(jnp.bfloat16)


def transform(field, matrix):
    halfway = jnp.einsum(
        "bcnm,cdmk->bdnk", field.astype(jnp.bfloat16), matrix, preferred_element_type=jnp.float32
    )
    return jnp.einsum(
        "cdkn,bcnm->bdkm", matrix, halfway.astype(jnp.bfloat16), preferred_element_type=jnp.float32
    )


def rotate(field, cosine, sine):
    real_part = field[:, 0]
    imag_part = field[:, 1]
    return jnp.stack(
        [real_part * cosine - imag_part * sine, real_part * sine + imag_part * cosine], axis=1
    )


def complex_mul(left, right):
    return jnp.stack(
        [
            left[:, 0] * right[:, 0] - left[:, 1] * right[:, 1],
            left[:, 0] * right[:, 1] + left[:, 1] * right[:, 0],
        ],
        axis=1,
    )


def conj_mul(left, right):
    return jnp.stack(
        [
            left[:, 0] * right[:, 0] + left[:, 1] * right[:, 1],
            left[:, 0] * right[:, 1] - left[:, 1] * right[:, 0],
        ],
        axis=1,
    )


def deposit(canvas, pieces, row_starts, col_starts):
    extent = pieces.shape[1:]
    for slot_index in range(pieces.shape[0]):
        corner = (0, 0, row_starts[slot_index], col_starts[slot_index])
        current = lax.dynamic_slice(canvas, corner, extent)
        canvas = lax.dynamic_update_slice(canvas, current + pieces[slot_index], corner)
    return canvas


def on_device(
    object_slices, probe_field, slice_phase, intensity, counts, chosen, row_offset, column_offset
):
    slice_count, _, height, breadth = object_slices.shape
    pattern = probe_field.shape[-1]
    slot_count = chosen.shape[1]
    cut_index = lax.axis_index("cuts")
    cut_total = lax.axis_size("cuts")
    forward_table = make_table(pattern, -1.0)
    inverse_table = make_table(pattern, 1.0)
    cosines = jnp.cos(slice_phase)
    sines = jnp.sin(slice_phase)
    picked = chosen[0]
    onehot = picked[:, None] == jnp.arange(row_offset.shape[1], dtype=jnp.int32)[None, :]
    row_starts = jnp.sum(jnp.where(onehot, row_offset[0][None, :], 0), axis=1)
    col_starts = jnp.sum(jnp.where(onehot, column_offset[0][None, :], 0), axis=1)
    is_live = jnp.arange(slot_count, dtype=jnp.int32) < counts[0]
    measured = jnp.take(intensity[0], picked, axis=0)
    extent = (slice_count, 2, pattern, pattern)
    neighbour = from_behind(object_slices.astype(jnp.bfloat16), "tile", -1).astype(
        object_slices.dtype
    )
    extended = jnp.concatenate([object_slices, neighbour], axis=3)

    def single(row_start, col_start):
        return lax.dynamic_slice(extended, (0, 0, row_start, col_start), extent)

    patches = jax.vmap(single)(row_starts, col_starts)
    groups = 1
    per_group = slot_count // groups
    turns = groups + cut_total - 1
    start_wave = jnp.broadcast_to(probe_field, (per_group, 2, pattern, pattern))

    def forward_turn(turn_index, carried):
        incoming, saved_in, saved_out = carried
        group_index = turn_index - cut_index
        is_valid = (group_index >= 0) & (group_index < groups)
        first_slot = jnp.clip(group_index, 0, groups - 1) * per_group
        current = jnp.where(cut_index == 0, start_wave, incoming.astype(jnp.float32))
        inputs = [current]
        product = complex_mul(current, patches[:, 0])
        spectrum = rotate(transform(product, forward_table), cosines[0], sines[0])
        outgoing = transform(spectrum, inverse_table).astype(jnp.bfloat16)
        stacked = jnp.stack(inputs, axis=1)
        previous_in = saved_in
        saved_in = lax.dynamic_update_slice_in_dim(
            saved_in, jnp.where(is_valid, stacked, previous_in), first_slot, 0
        )
        previous_out = saved_out
        saved_out = jnp.where(is_valid, outgoing, previous_out)
        incoming = from_behind(outgoing, "cuts", 1)
        return (incoming, saved_in, saved_out)

    forward_start = (
        jnp.zeros((per_group, 2, pattern, pattern), jnp.bfloat16),
        jnp.zeros((slot_count, slice_count, 2, pattern, pattern), jnp.float32),
        jnp.zeros((slot_count, 2, pattern, pattern), jnp.bfloat16),
    )
    _, saved_in, saved_out = lax.fori_loop(0, turns, forward_turn, forward_start)
    exit_wave = saved_out.astype(jnp.float32)
    power = exit_wave[:, 0] * exit_wave[:, 0] + exit_wave[:, 1] * exit_wave[:, 1]
    residual = jnp.where(
        is_live[:, None, None, None], 2.0 * (power - measured)[:, None] * exit_wave, 0.0
    )

    def backward_turn(turn_index, carried):
        incoming, slice_grads = carried
        group_index = turn_index - (cut_total - 1 - cut_index)
        is_valid = (group_index >= 0) & (group_index < groups)
        first_slot = jnp.clip(group_index, 0, groups - 1) * per_group
        cotangent = jnp.where(cut_index == cut_total - 1, residual, incoming.astype(jnp.float32))
        grads = [None] * slice_count
        for slice_index in reversed(range(slice_count)):
            spectrum = rotate(
                transform(cotangent, forward_table), cosines[slice_index], -sines[slice_index]
            )
            spread = transform(spectrum, inverse_table)
            grads[slice_index] = conj_mul(saved_in[:, slice_index], spread)
            cotangent = conj_mul(patches[:, slice_index], spread)
        stacked = jnp.stack(grads, axis=1)
        previous = slice_grads
        slice_grads = lax.dynamic_update_slice_in_dim(
            slice_grads, jnp.where(is_valid, stacked, previous), first_slot, 0
        )
        incoming = from_behind(cotangent.astype(jnp.bfloat16), "cuts", -1)
        return (incoming, slice_grads)

    backward_start = (
        jnp.zeros((per_group, 2, pattern, pattern), jnp.bfloat16),
        jnp.zeros((slot_count, slice_count, 2, pattern, pattern), jnp.float32),
    )
    _, slice_grads = lax.fori_loop(0, turns, backward_turn, backward_start)
    empty_canvas = jnp.zeros((slice_count, 2, height, 2 * breadth), jnp.float32)
    canvas = deposit(empty_canvas, slice_grads, row_starts, col_starts)
    carried = from_behind(canvas[..., breadth:].astype(jnp.bfloat16), "tile", 1).astype(jnp.float32)
    object_grad = canvas[..., :breadth] + carried
    return object_grad


def solution(mesh):
    return jax.shard_map(
        on_device,
        mesh=mesh,
        in_specs=(
            P("cuts", None, None, "tile"),
            P(),
            P("cuts", None, None),
            P("tile", None, None, None),
            P("tile"),
            P("tile", None),
            P("tile", None),
            P("tile", None),
        ),
        out_specs=P("cuts", None, None, "tile"),
        check_vma=False,
    )
```

profile of v0, /device:TPU:160, one launch (start us, length us, event | category | flops | bytes accessed | tf_op | source)
XLA Modules:
  0.0 310.9 jit_solution(12950722765228013526)
XLA Ops:
  0.0 3.9 %convert_element_type.165 = bf16[1,2,2048,256]{3,2,1,0:T(8,128)(2,1)} convert(f32[1,2,2048,256]{3,2,1,0:T(8,128)} %param.12) | non-fusion elementwise | flops 1048576 | bytes 6291456 | tf_op jit(solution)/shard_map/convert_element_type | solution.py:89
  3.9 7.5 %collective-permute-start.2 = (bf16[1,2,2048,256]{3,2,1,0:T(8,128)(2,1)}, bf16[1,2,2048,256]{3,2,1,0:T(8,128)(2,1)}, u32[]{:S(2)}, u32[]{:S(2)}) collective-permute-start(bf16[1,2,2048,256]{3,2,1,0:T(8,128)(2,1)} %convert_element_type.165), channel_id=1, source_target_pairs={{1,0},{2,1},{3,2},{4,3},{5,4},{6,5},{7,6},{8,7},{9,8},{10,9},{11,1... | collective-permute-start | bytes 6291464 | tf_op jit(solution)/shard_map/ppermute | solution.py:10
  44.4 12.3 %collective-permute-done.2 = bf16[1,2,2048,256]{3,2,1,0:T(8,128)(2,1)} collective-permute-done((bf16[1,2,2048,256]{3,2,1,0:T(8,128)(2,1)}, bf16[1,2,2048,256]{3,2,1,0:T(8,128)(2,1)}, u32[]{:S(2)}, u32[]{:S(2)}) %collective-permute-start.2) | collective-permute-done | bytes 2097184 | tf_op jit(solution)/shard_map/ppermute | solution.py:10
  58.6 4.6 %pad_maximum_fusion.1 = f32[1,2,2048,512]{3,2,1,0:T(8,128)} fusion(f32[1,2,2048,256]{3,2,1,0:T(8,128)S(1)} %convert_element_type.166, f32[1,2,2048,256]{3,2,1,0:T(8,128)S(1)} %copy-done.3), kind=kLoop, calls=%fused_computation.52 | loop fusion | flops 2097152 | bytes 16777216 | tf_op jit(solution)/shard_map/concatenate | solution.py:92
  63.2 23.6 %while.38 = (s32[]{:T(128)}, f32[1,2,2048,512]{3,2,1,0:T(8,128)}, s32[6,4]{0,1:T(4,128)S(1)}, f32[6,1,2,256,256]{4,3,2,1,0:T(8,128)}, s32[]{:T(128)}) while((s32[]{:T(128)}, f32[1,2,2048,512]{3,2,1,0:T(8,128)}, s32[6,4]{0,1:T(4,128)S(1)}, f32[6,1,2,256,256]{4,3,2,1,0:T(8,128)}, s32[]{:T(128)}) %tuple.132), condition=%wide.while_cond, body=%wide.while_body.sunk | while | flops 2 | bytes 1050225 | solution.py:95
  63.8 3.3 %bitcast_dynamic-update-slice_fusion.2 = f32[6,1,2,256,256]{4,3,2,1,0:T(8,128)} fusion(f32[6,1,2,256,256]{4,3,2,1,0:T(8,128)} %get-tuple-element.975, s32[]{:T(128)} %get-tuple-element.972, f32[1,2,2048,512]{3,2,1,0:T(8,128)} %get-tuple-element.978, s32[]{:T(128)} %bitcast.260, s32[]{:T(128)} %bitcast.261), kind=kLoop, calls=%fused_computation.2.clone.1 | loop fusion | bytes 1050112 | tf_op jit(solution)/shard_map/vmap()/gather
  67.7 3.3 %bitcast_dynamic-update-slice_fusion.2 = f32[6,1,2,256,256]{4,3,2,1,0:T(8,128)} fusion(f32[6,1,2,256,256]{4,3,2,1,0:T(8,128)} %get-tuple-element.975, s32[]{:T(128)} %get-tuple-element.972, f32[1,2,2048,512]{3,2,1,0:T(8,128)} %get-tuple-element.978, s32[]{:T(128)} %bitcast.260, s32[]{:T(128)} %bitcast.261), kind=kLoop, calls=%fused_computation.2.clone.1 | loop fusion | bytes 1050112 | tf_op jit(solution)/shard_map/vmap()/gather
  71.6 3.4 %bitcast_dynamic-update-slice_fusion.2 = f32[6,1,2,256,256]{4,3,2,1,0:T(8,128)} fusion(f32[6,1,2,256,256]{4,3,2,1,0:T(8,128)} %get-tuple-element.975, s32[]{:T(128)} %get-tuple-element.972, f32[1,2,2048,512]{3,2,1,0:T(8,128)} %get-tuple-element.978, s32[]{:T(128)} %bitcast.260, s32[]{:T(128)} %bitcast.261), kind=kLoop, calls=%fused_computation.2.clone.1 | loop fusion | bytes 1050112 | tf_op jit(solution)/shard_map/vmap()/gather
  75.6 3.3 %bitcast_dynamic-update-slice_fusion.2 = f32[6,1,2,256,256]{4,3,2,1,0:T(8,128)} fusion(f32[6,1,2,256,256]{4,3,2,1,0:T(8,128)} %get-tuple-element.975, s32[]{:T(128)} %get-tuple-element.972, f32[1,2,2048,512]{3,2,1,0:T(8,128)} %get-tuple-element.978, s32[]{:T(128)} %bitcast.260, s32[]{:T(128)} %bitcast.261), kind=kLoop, calls=%fused_computation.2.clone.1 | loop fusion | bytes 1050112 | tf_op jit(solution)/shard_map/vmap()/gather
  79.5 3.3 %bitcast_dynamic-update-slice_fusion.2 = f32[6,1,2,256,256]{4,3,2,1,0:T(8,128)} fusion(f32[6,1,2,256,256]{4,3,2,1,0:T(8,128)} %get-tuple-element.975, s32[]{:T(128)} %get-tuple-element.972, f32[1,2,2048,512]{3,2,1,0:T(8,128)} %get-tuple-element.978, s32[]{:T(128)} %bitcast.260, s32[]{:T(128)} %bitcast.261), kind=kLoop, calls=%fused_computation.2.clone.1 | loop fusion | bytes 1050112 | tf_op jit(solution)/shard_map/vmap()/gather
  83.4 3.3 %bitcast_dynamic-update-slice_fusion.2 = f32[6,1,2,256,256]{4,3,2,1,0:T(8,128)} fusion(f32[6,1,2,256,256]{4,3,2,1,0:T(8,128)} %get-tuple-element.975, s32[]{:T(128)} %get-tuple-element.972, f32[1,2,2048,512]{3,2,1,0:T(8,128)} %get-tuple-element.978, s32[]{:T(128)} %bitcast.260, s32[]{:T(128)} %bitcast.261), kind=kLoop, calls=%fused_computation.2.clone.1 | loop fusion | bytes 1050112 | tf_op jit(solution)/shard_map/vmap()/gather
  86.8 3.5 %copy.53 = f32[6,1,2,256,256]{3,4,2,0,1:T(8,128)} copy(f32[6,1,2,256,256]{4,3,2,1,0:T(8,128)} %get-tuple-element.655) | data formatting | bytes 6291456
  90.4 44.1 %while.39 = (s32[]{:T(128)}, bf16[6,2,256,256]{2,3,1,0:T(8,128)(2,1)S(1)}, f32[6,1,2,256,256]{4,3,2,0,1:T(8,128)}, bf16[6,2,256,256]{2,3,1,0:T(8,128)(2,1)}, pre...) while((s32[]{:T(128)}, ...), condition=%wide.region_3.4_spmd.clone, body=%wide.region_2.3_spmd.clone.sunk | while | flops 3242459136 | bytes 48234716 | solution.py:128
  92.5 2.4 subtract_convert_fusion.7
  95.0 4.7 %convolution_bitcast_fusion.6 = f32[6,2,256,256]{2,3,1,0:T(8,128)} fusion(bf16[6,1,256,256]{3,2,1,0:T(8,128)(2,1)S(1)} %get-tuple-element.943, bf16[6,1,256,256]{3,2,1,0:T(8,128)(2,1)S(1)} %get-tuple-element.944, bf16[2,2,256,256]{3,2,0,1:T(8,128)(2,1)} %get-tuple-element.1016), kind=kOutput, calls=%fused_computation.9.clone.1 | convolution fusion | flops 1614544896 | bytes 5242880 | tf_op jit(solution)/shard_map/while/body/eval_jaxpr/cdkn,bcnm->bdkm/dot_general | solution.py:28
  99.7 2.3 subtract_convert_fusion.8
  102.0 4.7 %select_select_fusion.2 = (bf16[6,2,256,256]{2,3,1,0:T(8,128)(2,1)}, bf16[6,2,256,256]{2,3,1,0:T(8,128)(2,1)}) fusion(bf16[6,2,256,256]{2,3,1,0:T(8,128)(2,1)} %get-tuple-element.999, pred[]{:T(512)S(6)} %compare.27, pred[]{:T(512)S(6)} %and.108, bf16[2,2,256,256]{3,2,0,1:T(8,128)(2,1)} %get-tuple-element.1019, ...), kind=kOutput, calls=%fused_computation.18.clone.1 | convolution fusion | flops 1616904192 | bytes 6815746 | tf_op jit(solution)/shard_map/while/body/eval_jaxpr/cdkn,bcnm->bdkm/dot_general | solution.py:28
  108.1 3.2 %bitcast_select_fusion.3 = f32[6,1,2,256,256]{4,3,2,0,1:T(8,128)} fusion(f32[6,1,2,256,256]{4,3,2,0,1:T(8,128)} %get-tuple-element.998, pred[]{:T(512)S(6)} %compare.27, pred[]{:T(512)S(6)} %and.108, bf16[6,2,256,256]{3,2,1,0:T(8,128)(2,1)S(1)} %copy.94, f32[2,256,256]{2,1,0:T(8,128)} %get-tuple-element.1021, pred[]{:T(512)} %get-tuple-element.1014), kind=kLoop, calls=%fused_computation.4.clone.1 | loop fusion | flops 3145728 | bytes 8388611 | tf_op jit(solution)/shard_map/while/body/eval_jaxpr/jit(_where)/select_n | solution.py:116
  113.4 2.4 subtract_convert_fusion.7
  115.8 4.7 %convolution_bitcast_fusion.6 = f32[6,2,256,256]{2,3,1,0:T(8,128)} fusion(bf16[6,1,256,256]{3,2,1,0:T(8,128)(2,1)S(1)} %get-tuple-element.943, bf16[6,1,256,256]{3,2,1,0:T(8,128)(2,1)S(1)} %get-tuple-element.944, bf16[2,2,256,256]{3,2,0,1:T(8,128)(2,1)} %get-tuple-element.1016), kind=kOutput, calls=%fused_computation.9.clone.1 | convolution fusion | flops 1614544896 | bytes 5242880 | tf_op jit(solution)/shard_map/while/body/eval_jaxpr/cdkn,bcnm->bdkm/dot_general | solution.py:28
  120.5 2.3 subtract_convert_fusion.8
  122.9 5.2 %select_select_fusion.2 = (bf16[6,2,256,256]{2,3,1,0:T(8,128)(2,1)}, bf16[6,2,256,256]{2,3,1,0:T(8,128)(2,1)}) fusion(bf16[6,2,256,256]{2,3,1,0:T(8,128)(2,1)} %get-tuple-element.999, pred[]{:T(512)S(6)} %compare.27, pred[]{:T(512)S(6)} %and.108, bf16[2,2,256,256]{3,2,0,1:T(8,128)(2,1)} %get-tuple-element.1019, ...), kind=kOutput, calls=%fused_computation.18.clone.1 | convolution fusion | flops 1616904192 | bytes 6815746 | tf_op jit(solution)/shard_map/while/body/eval_jaxpr/cdkn,bcnm->bdkm/dot_general | solution.py:28
  128.1 2.3 collective-permute-start
  130.4 4.2 %bitcast_select_fusion.3 = f32[6,1,2,256,256]{4,3,2,0,1:T(8,128)} fusion(f32[6,1,2,256,256]{4,3,2,0,1:T(8,128)} %get-tuple-element.998, pred[]{:T(512)S(6)} %compare.27, pred[]{:T(512)S(6)} %and.108, bf16[6,2,256,256]{3,2,1,0:T(8,128)(2,1)S(1)} %copy.94, f32[2,256,256]{2,1,0:T(8,128)} %get-tuple-element.1021, pred[]{:T(512)} %get-tuple-element.1014), kind=kLoop, calls=%fused_computation.4.clone.1 | loop fusion | flops 3145728 | bytes 8388611 | tf_op jit(solution)/shard_map/while/body/eval_jaxpr/jit(_where)/select_n | solution.py:116
  139.8 2.8 copy.54
  142.6 2.4 copy.56
  146.3 45.9 %while.40 = (s32[]{:T(128)}, bf16[6,2,256,256]{2,3,1,0:T(8,128)(2,1)}, f32[6,1,2,256,256]{3,4,2,0,1:T(8,128)}, f32[6,1,2,256,256]{3,4,2,0,1:T(8,128)}, pred[]{:T...) while((s32[]{:T(128)}, ...), condition=%wide.region_5.6_spmd.clone, body=%wide.region_4.5_spmd.clone.sunk | while | flops 3239313408 | bytes 50331864 | solution.py:161
  146.3 3.5 %convolution_bitcast_fusion.7 = f32[6,2,256,256]{2,3,1,0:T(8,128)S(1)} fusion(bf16[6,2,256,256]{2,3,1,0:T(8,128)(2,1)} %get-tuple-element.1057, bf16[6,2,256,256]{2,3,1,0:T(8,128)(2,1)} %get-tuple-element.1039, pred[]{:T(512)} %get-tuple-element.1056, bf16[2,2,256,256]{3,2,0,1:T(8,128)(2,1)} %get-tuple-element.1058), kind=kOutput, calls=%fused_computation.34.clone.1 | convolution fusion | flops 1612972032 | bytes 6815745 | tf_op jit(solution)/shard_map/while/body/eval_jaxpr/cdkn,bcnm->bdkm/dot_general | solution.py:28
  149.9 2.5 subtract_convert_fusion.9
  152.4 5.2 %convolution_bitcast_fusion.8 = f32[6,2,256,256]{2,3,1,0:T(8,128)} fusion(bf16[6,1,256,256]{2,3,1,0:T(8,128)(2,1)} %get-tuple-element.961, bf16[6,1,256,256]{2,3,1,0:T(8,128)(2,1)} %get-tuple-element.962, bf16[2,2,256,256]{3,2,0,1:T(8,128)(2,1)} %get-tuple-element.1061), kind=kOutput, calls=%fused_computation.33.clone.1 | convolution fusion | flops 1614544896 | bytes 5242880 | tf_op jit(solution)/shard_map/while/body/eval_jaxpr/cdkn,bcnm->bdkm/dot_general | solution.py:28
  157.6 4.7 %multiply_add_fusion.2 = (f32[6,1,256,256]{2,3,1,0:T(8,128)S(1)}, f32[6,1,256,256]{2,3,1,0:T(8,128)S(1)}, bf16[6,1,256,256]{2,3,1,0:T(8,128)(2,1)S(1)}, bf16[6,1,256,256]{2,3,1,0:T(8,128)(2,1)S(1)}) fusion(f32[6,2,256,256]{2,3,1,0:T(8,128)} %bitcast.290, f32[6,2,256,256]{2,3,1,0:T(8,128)} %convolution_bitcast_fusion.8, f32[6,2,256,256]{2,3,1,0:T(8,128)} %bitcast.293), kind=kLoop, calls=%fused_computation.43.clone.1 | loop fusion | flops 5505024 | bytes 14155776 | tf_op jit(solution)/shard_map/while/body/eval_jaxpr/add | solution.py:54
  167.1 2.2 collective-permute-done.1
  169.3 3.5 %convolution_bitcast_fusion.7 = f32[6,2,256,256]{2,3,1,0:T(8,128)S(1)} fusion(bf16[6,2,256,256]{2,3,1,0:T(8,128)(2,1)} %get-tuple-element.1057, bf16[6,2,256,256]{2,3,1,0:T(8,128)(2,1)} %get-tuple-element.1039, pred[]{:T(512)} %get-tuple-element.1056, bf16[2,2,256,256]{3,2,0,1:T(8,128)(2,1)} %get-tuple-element.1058), kind=kOutput, calls=%fused_computation.34.clone.1 | convolution fusion | flops 1612972032 | bytes 6815745 | tf_op jit(solution)/shard_map/while/body/eval_jaxpr/cdkn,bcnm->bdkm/dot_general | solution.py:28
  172.8 2.5 subtract_convert_fusion.9
  175.4 5.2 %convolution_bitcast_fusion.8 = f32[6,2,256,256]{2,3,1,0:T(8,128)} fusion(bf16[6,1,256,256]{2,3,1,0:T(8,128)(2,1)} %get-tuple-element.961, bf16[6,1,256,256]{2,3,1,0:T(8,128)(2,1)} %get-tuple-element.962, bf16[2,2,256,256]{3,2,0,1:T(8,128)(2,1)} %get-tuple-element.1061), kind=kOutput, calls=%fused_computation.33.clone.1 | convolution fusion | flops 1614544896 | bytes 5242880 | tf_op jit(solution)/shard_map/while/body/eval_jaxpr/cdkn,bcnm->bdkm/dot_general | solution.py:28
  180.6 4.7 %multiply_add_fusion.2 = (f32[6,1,256,256]{2,3,1,0:T(8,128)S(1)}, f32[6,1,256,256]{2,3,1,0:T(8,128)S(1)}, bf16[6,1,256,256]{2,3,1,0:T(8,128)(2,1)S(1)}, bf16[6,1,256,256]{2,3,1,0:T(8,128)(2,1)S(1)}) fusion(f32[6,2,256,256]{2,3,1,0:T(8,128)} %bitcast.290, f32[6,2,256,256]{2,3,1,0:T(8,128)} %convolution_bitcast_fusion.8, f32[6,2,256,256]{2,3,1,0:T(8,128)} %bitcast.293), kind=kLoop, calls=%fused_computation.43.clone.1 | loop fusion | flops 5505024 | bytes 14155776 | tf_op jit(solution)/shard_map/while/body/eval_jaxpr/add | solution.py:54
  187.9 4.0 %fusion.89 = f32[6,1,2,256,256]{3,4,2,0,1:T(8,128)} fusion(f32[6,1,256,256]{2,3,1,0:T(8,128)S(1)} %get-tuple-element.965, f32[6,1,256,256]{2,3,1,0:T(8,128)S(1)} %get-tuple-element.966, f32[6,1,2,256,256]{3,4,2,0,1:T(8,128)} %get-tuple-element.1040, pred[]{:T(512)S(6)} %compare.28, pred[]{:T(512)S(6)} %and.109), kind=kLoop, calls=%fused_computation.29.clone.1 | loop fusion | flops 2359296 | bytes 9437186 | tf_op jit(solution)/shard_map/while/body/eval_jaxpr/jit(_where)/select_n | solution.py:152
  192.2 2.4 copy.57
  195.4 4.3 %broadcast_in_dim.63 = f32[1,2,2048,512]{3,2,1,0:T(8,128)} broadcast(f32[]{:T(128)} %constant.97.clone.1), dimensions={} | broadcast | bytes 8388612 | tf_op jit(solution)/shard_map/broadcast_in_dim | solution.py:162
  199.8 6.6 %dynamic_update_slice.24 = f32[1,2,2048,512]{3,2,1,0:T(8,128)} dynamic-update-slice(f32[1,2,2048,512]{3,2,1,0:T(8,128)} %broadcast_in_dim.63, f32[1,2,256,256]{3,2,1,0:T(8,128)} %slice_bitcast_fusion.5, s32[]{:T(128)} %constant.98.clone.1, s32[]{:T(128)} %constant.98.clone.1, s32[]{:T(128)S(6)} %select_n.255, s32[]{:T(128)S(6)} %select_n.256) | dynamic-update-slice | bytes 1048580 | tf_op jit(solution)/shard_map/dynamic_update_slice | solution.py:66
  208.5 6.6 %dynamic_update_slice.25 = f32[1,2,2048,512]{3,2,1,0:T(8,128)} dynamic-update-slice(f32[1,2,2048,512]{3,2,1,0:T(8,128)} %dynamic_update_slice.24, f32[1,2,256,256]{3,2,1,0:T(8,128)} %fusion.45, s32[]{:T(128)} %constant.98.clone.1, s32[]{:T(128)} %constant.98.clone.1, s32[]{:T(128)S(6)} %select_n.257, s32[]{:T(128)S(6)} %select_n.258) | dynamic-update-slice | bytes 1048580 | tf_op jit(solution)/shard_map/dynamic_update_slice | solution.py:66
  217.3 6.7 %dynamic_update_slice.26 = f32[1,2,2048,512]{3,2,1,0:T(8,128)} dynamic-update-slice(f32[1,2,2048,512]{3,2,1,0:T(8,128)} %dynamic_update_slice.25, f32[1,2,256,256]{3,2,1,0:T(8,128)} %fusion.44, s32[]{:T(128)} %constant.98.clone.1, s32[]{:T(128)} %constant.98.clone.1, s32[]{:T(128)S(6)} %select_n.259, s32[]{:T(128)S(6)} %select_n.260) | dynamic-update-slice | bytes 1048580 | tf_op jit(solution)/shard_map/dynamic_update_slice | solution.py:66
  226.2 6.6 %dynamic_update_slice.27 = f32[1,2,2048,512]{3,2,1,0:T(8,128)} dynamic-update-slice(f32[1,2,2048,512]{3,2,1,0:T(8,128)} %dynamic_update_slice.26, f32[1,2,256,256]{3,2,1,0:T(8,128)} %fusion.43, s32[]{:T(128)} %constant.98.clone.1, s32[]{:T(128)} %constant.98.clone.1, s32[]{:T(128)S(6)} %select_n.261, s32[]{:T(128)S(6)} %select_n.262) | dynamic-update-slice | bytes 1048580 | tf_op jit(solution)/shard_map/dynamic_update_slice | solution.py:66
  234.9 6.6 %dynamic_update_slice.28 = f32[1,2,2048,512]{3,2,1,0:T(8,128)} dynamic-update-slice(f32[1,2,2048,512]{3,2,1,0:T(8,128)} %dynamic_update_slice.27, f32[1,2,256,256]{3,2,1,0:T(8,128)} %fusion.42, s32[]{:T(128)} %constant.98.clone.1, s32[]{:T(128)} %constant.98.clone.1, s32[]{:T(128)S(6)} %select_n.263, s32[]{:T(128)S(6)} %select_n.264) | dynamic-update-slice | bytes 1048580 | tf_op jit(solution)/shard_map/dynamic_update_slice | solution.py:66
  243.7 6.6 %dynamic_update_slice.29 = f32[1,2,2048,512]{3,2,1,0:T(8,128)} dynamic-update-slice(f32[1,2,2048,512]{3,2,1,0:T(8,128)} %dynamic_update_slice.28, f32[1,2,256,256]{3,2,1,0:T(8,128)} %fusion.41, s32[]{:T(128)} %constant.98.clone.1, s32[]{:T(128)} %constant.98.clone.1, s32[]{:T(128)S(6)} %select_n.265, s32[]{:T(128)S(6)} %select_n.266) | dynamic-update-slice | bytes 1048580 | tf_op jit(solution)/shard_map/dynamic_update_slice | solution.py:66
  250.4 2.4 slice.346
  254.7 51.4 %collective-permute-done.3 = bf16[1,2,2048,256]{3,2,1,0:T(8,128)(2,1)S(1)} collective-permute-done((bf16[1,2,2048,256]{3,2,1,0:T(8,128)(2,1)S(1)}, bf16[1,2,2048,256]{3,2,1,0:T(8,128)(2,1)S(1)}, u32[]{:S(2)}, u32[]{:S(2)}) %collective-permute-start.3) | collective-permute-done | bytes 2097184 | tf_op jit(solution)/shard_map/ppermute | solution.py:10
  306.0 4.9 %slice_add_fusion = f32[1,2,2048,256]{3,2,1,0:T(8,128)} fusion(f32[1,2,2048,512]{3,2,1,0:T(8,128)} %dynamic_update_slice.29, bf16[1,2,2048,256]{3,2,1,0:T(8,128)(2,1)S(1)} %collective-permute-done.3), kind=kLoop, calls=%fused_computation.54 | loop fusion | flops 2097152 | bytes 10485760 | tf_op jit(solution)/shard_map/add | solution.py:165
  (84 shorter events, 48.5 us)
Async XLA Ops:
  0.0 34.2 %copy-start = (f32[1,8,256,256]{3,2,1,0:T(8,128)S(1)}, f32[1,8,256,256]{3,2,1,0:T(8,128)}, u32[]{:S(2)}) copy-start(f32[1,8,256,256]{3,2,1,0:T(8,128)} %param.15) | copy-start | bytes 6291460
  0.0 11.5 %copy-start.9 = (s32[1,6]{1,0:T(1,128)S(1)}, s32[1,6]{1,0:T(1,128)}, u32[]{:S(2)}) copy-start(s32[1,6]{1,0:T(1,128)} %param.17) | copy-start | bytes 76
  0.0 11.5 %copy-start.7 = (s32[1,8]{1,0:T(1,128)S(1)}, s32[1,8]{1,0:T(1,128)}, u32[]{:S(2)}) copy-start(s32[1,8]{1,0:T(1,128)} %param.18) | copy-start | bytes 100
  0.0 11.5 %copy-start.8 = (s32[1,8]{1,0:T(1,128)S(1)}, s32[1,8]{1,0:T(1,128)}, u32[]{:S(2)}) copy-start(s32[1,8]{1,0:T(1,128)} %param.19) | copy-start | bytes 100
  3.9 52.7 %collective-permute-start.2 = (bf16[1,2,2048,256]{3,2,1,0:T(8,128)(2,1)}, bf16[1,2,2048,256]{3,2,1,0:T(8,128)(2,1)}, u32[]{:S(2)}, u32[]{:S(2)}) collective-permute-start(bf16[1,2,2048,256]{3,2,1,0:T(8,128)(2,1)} %convert_element_type.165), channel_id=1, source_target_pairs={{1,0},{2,1},{3,2},{4,3},{5,4},{6,5},{7,6},{8,7},{9,8},{10,9},{11,1... | collective-permute-start | bytes 6291464 | tf_op jit(solution)/shard_map/ppermute | solution.py:10
  30.6 1.0 copy-start.6
  33.4 2.6 copy-start.4
  44.4 14.2 %copy-start.3 = (f32[1,2,2048,256]{3,2,1,0:T(8,128)S(1)}, f32[1,2,2048,256]{3,2,1,0:T(8,128)}, u32[]{:S(2)}) copy-start(f32[1,2,2048,256]{3,2,1,0:T(8,128)} %param.12) | copy-start | bytes 12582916
  106.7 4.6 %collective-permute-start = (bf16[6,2,256,256]{2,3,1,0:T(8,128)(2,1)}, bf16[6,2,256,256]{2,3,1,0:T(8,128)(2,1)S(1)}, u32[]{:S(2)}, u32[]{:S(2)}) collective-permute-start(bf16[6,2,256,256]{2,3,1,0:T(8,128)(2,1)} %get-tuple-element.947), channel_id=1, source_target_pairs={{0,128},{1,129},{2,130},{3,131},{4,132},{5,133},{6,134},{7,135},{8... | collective-permute-start | bytes 4718600 | tf_op jit(solution)/shard_map/while/body/eval_jaxpr/ppermute | solution.py:10
  128.1 6.4 %collective-permute-start = (bf16[6,2,256,256]{2,3,1,0:T(8,128)(2,1)}, bf16[6,2,256,256]{2,3,1,0:T(8,128)(2,1)S(1)}, u32[]{:S(2)}, u32[]{:S(2)}) collective-permute-start(bf16[6,2,256,256]{2,3,1,0:T(8,128)(2,1)} %get-tuple-element.947), channel_id=1, source_target_pairs={{0,128},{1,129},{2,130},{3,131},{4,132},{5,133},{6,134},{7,135},{8... | collective-permute-start | bytes 4718600 | tf_op jit(solution)/shard_map/while/body/eval_jaxpr/ppermute | solution.py:10
  136.3 1.4 copy-start.5
  139.8 2.8 copy-start.2
  163.7 5.6 %collective-permute-start.1 = (bf16[6,2,256,256]{2,3,1,0:T(8,128)(2,1)}, bf16[6,2,256,256]{2,3,1,0:T(8,128)(2,1)}, u32[]{:S(2)}, u32[]{:S(2)}) collective-permute-start(bf16[6,2,256,256]{2,3,1,0:T(8,128)(2,1)} %pad_maximum_fusion.9), channel_id=1, source_target_pairs={{128,0},{129,1},{130,2},{131,3},{132,4},{133,5},{134,6},{135,7},{1... | collective-permute-start | bytes 4718600 | tf_op jit(solution)/shard_map/while/body/eval_jaxpr/ppermute | solution.py:10
  186.6 5.6 %collective-permute-start.1 = (bf16[6,2,256,256]{2,3,1,0:T(8,128)(2,1)}, bf16[6,2,256,256]{2,3,1,0:T(8,128)(2,1)}, u32[]{:S(2)}, u32[]{:S(2)}) collective-permute-start(bf16[6,2,256,256]{2,3,1,0:T(8,128)(2,1)} %pad_maximum_fusion.9), channel_id=1, source_target_pairs={{128,0},{129,1},{130,2},{131,3},{132,4},{133,5},{134,6},{135,7},{1... | collective-permute-start | bytes 4718600 | tf_op jit(solution)/shard_map/while/body/eval_jaxpr/ppermute | solution.py:10
  252.7 53.3 %collective-permute-start.3 = (bf16[1,2,2048,256]{3,2,1,0:T(8,128)(2,1)S(1)}, bf16[1,2,2048,256]{3,2,1,0:T(8,128)(2,1)S(1)}, u32[]{:S(2)}, u32[]{:S(2)}) collective-permute-start(bf16[1,2,2048,256]{3,2,1,0:T(8,128)(2,1)S(1)} %slice.346), channel_id=1, source_target_pairs={{0,1},{1,2},{2,3},{3,4},{4,5},{5,6},{6,7},{7,8},{8,9},{9,10},{10,1... | collective-permute-start | bytes 6291464 | tf_op jit(solution)/shard_map/ppermute | solution.py:10
  306.0 4.9 %copy-start.1 = (f32[1,8,256,256]{3,2,1,0:T(8,128)S(1)}, f32[1,8,256,256]{3,2,1,0:T(8,128)}, u32[]{:S(2)}) copy-start(f32[1,8,256,256]{3,2,1,0:T(8,128)} %param.15) | copy-start | bytes 6291460
where the time goes:
time: 316 us; the launch traced here: 311 us
  local copies, waits for them, and re-layouts  92.2 us (29%)
  other arithmetic  76.5 us (24%)
  waiting for transfers between devices  66.1 us (21%)
  matrix products  36.9 us (12%)
  between operations  23.3 us (7%)
  starting transfers between devices  15.7 us (5%)
    ppermute x6, waiting for transfers between devices, from_behind(): lax.ppermute(value, axis, [(source, source + steps) for source in range(f...  66.1 us
    dynamic_update_slice x6, local copies, waits for them, and re-layouts, deposit(): lax.dynamic_update_slice(canvas, current + pieces[slot_index], corner)  39.8 us
    dot_general x8, matrix products, transform(): jnp.einsum('cdkn,bcnm->bdkm', matrix, halfway.astype(jnp.bfloat16), prefe...  36.9 us
    gather x18, local copies, waits for them, and re-layouts  23.6 us
    another operation x10, other arithmetic  17.8 us
    ppermute x6, starting transfers between devices, from_behind(): lax.ppermute(value, axis, [(source, source + steps) for source in range(f...  15.7 us
    unnamed x25, local copies, waits for them, and re-layouts  10.8 us
    add x5, other arithmetic, deposit(): current + pieces[slot_index]  10.7 us
  transfers between devices with their start and end apart: 6, of which 4 were waited for; matrix products, arithmetic and copies ran while one was open for 7% of the time, Pallas kernels for 0%

commit v1 on v0

v1 whole, which is shorter than its diff:
```python
import jax
import jax.numpy as jnp
import numpy as np
from jax import lax
from jax.experimental import pallas as pl
from jax.experimental.pallas import tpu as pltpu
from jax.sharding import PartitionSpec as P

BF16 = jnp.bfloat16
F32 = jnp.float32


def dft_tables(length):
    index = np.arange(length, dtype=np.int32)
    product = index[:, None] * index[None, :] % length
    angle = product.astype(np.float32) * np.float32(2.0 * np.pi / length)
    scale = np.float32(length ** (-0.5))
    cosine = np.cos(angle) * scale
    sine = np.sin(angle) * scale
    forward = np.block([[cosine, -sine], [sine, cosine]])
    inverse = np.block([[cosine, sine], [-sine, cosine]])
    return forward.astype(BF16), inverse.astype(BF16)


def iota(shape, axis):
    return lax.broadcasted_iota(jnp.int32, shape, axis)


def slot_kernel(
    counts, chosen, row_offset, column_offset,
    obj_hbm, probe_hbm, phase_hbm, intensity_hbm, fwd_hbm, inv_hbm,
    index_out, own_out, halo_out,
    obj, probe, phase, trig, intensity, fwd, inv,
    own, own_send, halo, halo_send, terms, psi0, psi1, window, xbuf, ybuf,
    index_send, index_recv,
    in_sem, index_sem, phase_sem, own_ssem, own_rsem, halo_ssem, halo_rsem,
    out_sem, part_ssem, part_rsem, edge_ssem, edge_rsem,
):
    slots = chosen.shape[1]
    pairs = slots // 2
    size = probe.shape[-1]
    last_block = obj.shape[1] - 1
    core = lax.axis_index("cuts")
    tile = lax.axis_index("tile")
    tiles = lax.axis_size("tile")
    other = 1 - core
    right = lax.rem(tile + 1, tiles)
    left = lax.rem(tile + tiles - 1, tiles)

    loads = [
        pltpu.make_async_copy(obj_hbm, obj, in_sem.at[0]),
        pltpu.make_async_copy(phase_hbm, phase.at[core], in_sem.at[1]),
        pltpu.make_async_copy(probe_hbm, probe, in_sem.at[2]),
        pltpu.make_async_copy(fwd_hbm, fwd, in_sem.at[3]),
        pltpu.make_async_copy(inv_hbm, inv, in_sem.at[4]),
        pltpu.make_async_copy(intensity_hbm, intensity, in_sem.at[5]),
    ]
    for load in loads:
        load.start()

    barrier = pltpu.get_barrier_semaphore()
    peers = [{"cuts": other, "tile": tile}]
    for there in (left, right):
        for cut in (0, 1):
            peers.append({"cuts": cut, "tile": there})
    for peer in peers:
        pl.semaphore_signal(barrier, inc=1, device_id=peer)
    for j in range(slots):
        q = chosen[0, j]
        index_send[j] = row_offset[0, q]
        index_send[8 + j] = column_offset[0, q]
        index_send[16 + j] = (j < counts[0]).astype(jnp.int32)
    for j in list(range(slots, 8)) + list(range(8 + slots, 16)) + list(range(16 + slots, 32)):
        index_send[j] = 0
    pl.semaphore_wait(barrier, len(peers))

    index_copy = pltpu.make_async_remote_copy(
        index_send, index_recv, index_sem.at[0], index_sem.at[1],
        device_id={"cuts": core, "tile": right},
    )
    index_copy.start()
    loads[1].wait()
    phase_copy = pltpu.make_async_remote_copy(
        phase.at[core], phase.at[core], phase_sem.at[0], phase_sem.at[1],
        device_id={"cuts": other, "tile": tile},
    )
    phase_copy.start()
    loads[0].wait()
    index_copy.wait_recv()

    rows = iota((size, size), 0)
    lanes = iota((size, size), 1)

    def fold(row, plane):
        block = lax.shift_right_logical(row, 8)
        after = jnp.minimum(block + 1, last_block)
        here = obj[plane, block]
        below = obj[plane, after]
        return jnp.where(rows >= jnp.bitwise_and(row, size - 1), here, below).astype(BF16)

    def halo_copy(i, half):
        j = 2 * i + half
        return pltpu.make_async_remote_copy(
            halo_send.at[j], halo.at[i, core], halo_ssem.at[j], halo_rsem.at[i, core],
            device_id={"cuts": half, "tile": left},
        )

    def own_copy(i):
        return pltpu.make_async_remote_copy(
            own_send.at[i], own.at[i, core], own_ssem.at[i], own_rsem.at[i],
            device_id={"cuts": other, "tile": tile},
        )

    @pl.loop(0, pairs)
    def _(i):
        for half in (0, 1):
            row = index_recv[2 * i + half]
            for plane in (0, 1):
                halo_send[2 * i + half, plane] = fold(row, plane)
            halo_copy(i, half).start()

    @pl.loop(0, pairs)
    def _(i):
        row = index_send[2 * i + other]
        for plane in (0, 1):
            own_send[i, plane] = fold(row, plane)
        own_copy(i).start()
        row = index_send[2 * i + core]
        for plane in (0, 1):
            own[i, core, plane] = fold(row, plane)

    for k in range(32):
        index_out[k] = index_send[k]
        index_out[32 + k] = index_recv[k]

    phase_copy.wait_recv()

    @pl.loop(0, 2 * size // 32)
    def _(k):
        cut = k // (size // 32)
        start = pl.multiple_of(lax.rem(k, size // 32) * 32, 32)
        angle = phase[cut, pl.ds(start, 32), :]
        trig[cut, 0, pl.ds(start, 32), :] = jnp.cos(angle)
        trig[cut, 1, pl.ds(start, 32), :] = jnp.sin(angle)

    for load in loads[2:]:
        load.wait()

    def stage(real, imag):
        xbuf[:, :size] = real.astype(BF16)
        xbuf[:, size:] = imag.astype(BF16)

    def transform(right_table, left_table):
        halfway = jnp.dot(xbuf[...], right_table[...], preferred_element_type=F32)
        ybuf[:size, :] = halfway[:, :size].astype(BF16)
        ybuf[size:, :] = halfway[:, size:].astype(BF16)
        field = jnp.dot(left_table[...], ybuf[...], preferred_element_type=F32)
        return field[:size], field[size:]

    def propagate(real, imag, cut, sign):
        stage(real, imag)
        real, imag = transform(fwd, inv)
        cosine = trig[cut, 0]
        sine = trig[cut, 1] * sign
        stage(real * cosine - imag * sine, real * sine + imag * cosine)
        return transform(inv, fwd)

    def edge_copy(i, cut):
        j = 2 * i + core
        return pltpu.make_async_remote_copy(
            terms.at[i, cut], halo_out.at[j], edge_ssem.at[i, cut], edge_rsem.at[j],
            device_id={"cuts": cut, "tile": right},
        )

    def part_copy(i):
        j = 2 * i + core
        return pltpu.make_async_remote_copy(
            terms.at[i, other], own_out.at[j], part_ssem.at[i], part_rsem.at[i],
            device_id={"cuts": other, "tile": tile},
        )

    def keep_copy(i):
        return pltpu.make_async_copy(terms.at[i, core], own_out.at[2 * i + core], out_sem.at[i])

    @pl.loop(0, pairs)
    def _(i):
        j = 2 * i + core
        position = chosen[0, j]
        row = jnp.bitwise_and(row_offset[0, position], size - 1)
        column = column_offset[0, position]

        to_row = (rows == jnp.bitwise_and(lanes + row, size - 1)).astype(F32).astype(BF16)
        to_lane = (lanes == jnp.bitwise_and(rows + column, size - 1)).astype(F32).astype(BF16)

        def moved(value):
            moving = jnp.dot(value, to_lane, preferred_element_type=F32).astype(BF16)
            return jnp.dot(to_row, moving, preferred_element_type=F32)

        def shifted(value):
            high = value.astype(BF16)
            low = (value - high.astype(F32)).astype(BF16)
            return moved(high) + moved(low)

        for plane in (0, 1):
            psi0[plane] = shifted(probe[plane])
        own_copy(i).wait_recv()
        inside = lanes >= column
        scale = (tile < tiles - 1).astype(F32)
        for cut in (0, 1):
            pltpu.make_async_remote_copy(
                halo_send.at[0], halo.at[i, cut], halo_ssem.at[0], halo_rsem.at[i, cut],
                device_id={"cuts": cut, "tile": right},
            ).wait_recv()
            for plane in (0, 1):
                window[cut, plane] = jnp.where(
                    inside, own[i, cut, plane].astype(F32), halo[i, cut, plane].astype(F32) * scale
                )

        real, imag = psi0[0], psi0[1]
        o_real, o_imag = window[0, 0], window[0, 1]
        real, imag = propagate(real * o_real - imag * o_imag, real * o_imag + imag * o_real, 0, 1.0)
        psi1[0] = real.astype(BF16)
        psi1[1] = imag.astype(BF16)
        real, imag = psi1[0].astype(F32), psi1[1].astype(F32)
        o_real, o_imag = window[1, 0], window[1, 1]
        real, imag = propagate(real * o_real - imag * o_imag, real * o_imag + imag * o_real, 1, 1.0)
        real, imag = real.astype(BF16).astype(F32), imag.astype(BF16).astype(F32)
        factor = 2.0 * (real * real + imag * imag - shifted(intensity[position]))
        live = j < counts[0]
        real = jnp.where(live, factor * real, 0.0)
        imag = jnp.where(live, factor * imag, 0.0)

        real, imag = propagate(real, imag, 1, -1.0)
        w_real, w_imag = psi1[0].astype(F32), psi1[1].astype(F32)
        terms[i, 1, 0] = (w_real * real + w_imag * imag).astype(BF16)
        terms[i, 1, 1] = (w_real * imag - w_imag * real).astype(BF16)
        edge_copy(i, 1).start()
        o_real, o_imag = window[1, 0], window[1, 1]
        real, imag = propagate(
            o_real * real + o_imag * imag, o_real * imag - o_imag * real, 0, -1.0
        )
        w_real, w_imag = psi0[0], psi0[1]
        terms[i, 0, 0] = (w_real * real + w_imag * imag).astype(BF16)
        terms[i, 0, 1] = (w_real * imag - w_imag * real).astype(BF16)
        edge_copy(i, 0).start()
        part_copy(i).start()
        keep_copy(i).start()

    index_copy.wait_send()
    phase_copy.wait_send()

    @pl.loop(0, pairs)
    def _(i):
        own_copy(i).wait_send()
        part_copy(i).wait_send()
        part_copy(i).wait_recv()
        keep_copy(i).wait()
        for half in (0, 1):
            halo_copy(i, half).wait_send()
            edge_copy(i, half).wait_send()
            pltpu.make_async_remote_copy(
                terms.at[0, 0], halo_out.at[2 * i + half], edge_ssem.at[0, 0], edge_rsem.at[2 * i + half],
                device_id={"cuts": core, "tile": right},
            ).wait_recv()


def deposit_kernel(index, own_ref, halo_ref, out_ref):
    block = pl.program_id(0)
    slots = own_ref.shape[0]
    size = out_ref.shape[-1]
    rows = iota((size, size), 0)
    lanes = iota((size, size), 1)
    has_left = lax.axis_index("tile") > 0
    out_ref[...] = jnp.zeros_like(out_ref)

    for base, ref in ((0, own_ref), (32, halo_ref)):

        @pl.loop(0, slots)
        def _(j, base=base, ref=ref):
            row = index[base + j]
            column = index[base + 8 + j]
            first = lax.shift_right_logical(row, 8)
            start = jnp.bitwise_and(row, size - 1)
            live = index[base + 16 + j] > 0
            if base:
                live = live & has_left

            @pl.when(live & ((first == block) | (first + 1 == block)))
            def _():
                above = first == block
                low = jnp.where(above, start, 0)
                high = jnp.where(above, size, start)
                mask = (rows >= low) & (rows < high)
                mask = mask & ((lanes < column) if base else (lanes >= column))
                for plane in (0, 1):
                    out_ref[plane] += jnp.where(mask, ref[j, plane].astype(F32), 0.0)


def on_device(
    object_slices, probe_field, slice_phase, intensity, counts, chosen, row_offset, column_offset
):
    _, _, height, breadth = object_slices.shape
    size = probe_field.shape[-1]
    scan = row_offset.shape[1]
    slots = chosen.shape[1]
    pairs = slots // 2
    forward, inverse = dft_tables(size)
    smem = pl.BlockSpec(memory_space=pltpu.SMEM)
    anywhere = pl.BlockSpec(memory_space=pl.ANY)
    plane = (size, size)
    terms_shape = jax.ShapeDtypeStruct((slots, 2) + plane, BF16)
    dma = pltpu.SemaphoreType.DMA
    index, own, halo = pl.pallas_call(
        slot_kernel,
        out_shape=(jax.ShapeDtypeStruct((64,), jnp.int32), terms_shape, terms_shape),
        in_specs=[smem] * 4 + [anywhere] * 6,
        out_specs=(smem, anywhere, anywhere),
        scratch_shapes=[
            pltpu.VMEM((2, height // size) + plane, F32),
            pltpu.VMEM((2,) + plane, F32),
            pltpu.VMEM((2,) + plane, F32),
            pltpu.VMEM((2, 2) + plane, F32),
            pltpu.VMEM((scan,) + plane, F32),
            pltpu.VMEM((2 * size, 2 * size), BF16),
            pltpu.VMEM((2 * size, 2 * size), BF16),
            pltpu.VMEM((pairs, 2, 2) + plane, BF16),
            pltpu.VMEM((pairs, 2) + plane, BF16),
            pltpu.VMEM((pairs, 2, 2) + plane, BF16),
            pltpu.VMEM((slots, 2) + plane, BF16),
            pltpu.VMEM((pairs, 2, 2) + plane, BF16),
            pltpu.VMEM((2,) + plane, F32),
            pltpu.VMEM((2,) + plane, BF16),
            pltpu.VMEM((2, 2) + plane, F32),
            pltpu.VMEM((size, 2 * size), BF16),
            pltpu.VMEM((2 * size, size), BF16),
            pltpu.SMEM((32,), jnp.int32),
            pltpu.SMEM((32,), jnp.int32),
            dma((6,)),
            dma((2,)),
            dma((2,)),
            dma((pairs,)),
            dma((pairs,)),
            dma((slots,)),
            dma((pairs, 2)),
            dma((pairs,)),
            dma((pairs,)),
            dma((pairs,)),
            dma((pairs, 2)),
            dma((slots,)),
        ],
        compiler_params=pltpu.CompilerParams(
            collective_id=0, has_side_effects=True, vmem_limit_bytes=48 * 1024 * 1024
        ),
        name="slots",
    )(
        counts, chosen, row_offset, column_offset,
        object_slices.reshape(2, height // size, size, breadth), probe_field, slice_phase[0], intensity[0],
        jnp.asarray(forward), jnp.asarray(inverse),
    )
    resident = pl.BlockSpec(
        (slots, 2) + plane, lambda b, *_: (0, 0, 0, 0), pipeline_mode=pl.Buffered(1)
    )
    gradient = pl.pallas_call(
        deposit_kernel,
        grid_spec=pltpu.PrefetchScalarGridSpec(
            num_scalar_prefetch=1,
            grid=(height // size,),
            in_specs=[resident, resident],
            out_specs=pl.BlockSpec((2, size, breadth), lambda b, *_: (0, b, 0)),
        ),
        out_shape=jax.ShapeDtypeStruct((2, height, breadth), F32),
        compiler_params=pltpu.CompilerParams(vmem_limit_bytes=32 * 1024 * 1024),
        name="deposit",
    )(index, own, halo)
    return gradient[None]


def solution(mesh):
    return jax.shard_map(
        on_device,
        mesh=mesh,
        in_specs=(
            P("cuts", None, None, "tile"),
            P(),
            P("cuts", None, None),
            P("tile", None, None, None),
            P("tile"),
            P("tile", None),
            P("tile", None),
            P("tile", None),
        ),
        out_specs=P("cuts", None, None, "tile"),
        check_vma=False,
    )
```

time: 316 us -> 79.1 us (0.25)
  the two profiles are of different devices: /device:TPU:160 before, /device:TPU:0 now
where the time goes in v1:
time: 79.1 us; the launch traced here: 78.9 us
  Pallas kernels  72.2 us (91%)
  local copies, waits for them, and re-layouts  6.03 us (8%)
    pallas_call x1, Pallas kernels, on_device(): pl.pallas_call(slot_kernel, out_shape=(jax.ShapeDtypeStruct((64,), jnp.in...  66.9 us
    unnamed x14, local copies, waits for them, and re-layouts  6.03 us
    pallas_call x1, Pallas kernels, on_device(): pl.pallas_call(deposit_kernel, grid_spec=pltpu.PrefetchScalarGridSpec(num...  5.24 us

profile of v1, /device:TPU:0, one launch (start us, length us, event | category | flops | bytes accessed | tf_op | source)
XLA Modules:
  0.0 78.9 jit_solution(12248676980484270241)
XLA Ops:
  0.7 0.0 copy-start
  0.7 1.0 %copy-done = f32[2,256,256]{2,1,0:T(8,128)S(1)} copy-done((f32[2,256,256]{2,1,0:T(8,128)S(1)}, f32[2,256,256]{2,1,0:T(8,128)}, u32[]{:S(2)}) %copy-start) | copy-done | bytes 524312
  1.7 0.0 copy-start.1
  1.7 1.0 %copy-done.1 = bf16[512,512]{1,0:T(8,128)(2,1)S(1)} copy-done((bf16[512,512]{1,0:T(8,128)(2,1)S(1)}, bf16[512,512]{1,0:T(8,128)(2,1)}, u32[]{:S(2)}) %copy-start.1) | copy-done | bytes 524312
  2.7 0.0 copy-start.2
  2.7 1.0 %copy-done.2 = bf16[512,512]{1,0:T(8,128)(2,1)S(1)} copy-done((bf16[512,512]{1,0:T(8,128)(2,1)S(1)}, bf16[512,512]{1,0:T(8,128)(2,1)}, u32[]{:S(2)}) %copy-start.2) | copy-done | bytes 524312
  3.8 0.0 copy-start.3
  3.8 0.9 %copy-done.3 = f32[1,256,256]{2,1,0:T(8,128)S(1)} copy-done((f32[1,256,256]{2,1,0:T(8,128)S(1)}, f32[1,256,256]{2,1,0:T(8,128)}, u32[]{:S(2)}) %copy-start.3) | copy-done | bytes 262168
  4.7 0.0 copy-start.4
  4.7 0.7 copy-done.4
  5.4 0.0 copy-start.5
  5.4 0.7 copy-done.5
  6.0 0.0 copy-start.6
  6.0 0.7 copy-done.6
  6.7 66.9 %slots.1 = (s32[64]{0:T(128)S(1)}, bf16[6,2,256,256]{3,2,1,0:T(8,128)(2,1)S(1)}, bf16[6,2,256,256]{3,2,1,0:T(8,128)(2,1)S(1)}) custom-call(s32[1]{0:T(128)S(6)} %copy.11.counts, s32[1,6]{1,0:T(1,128)S(1)} %copy-done.4, s32[1,8]{1,0:T(1,128)S(1)} %copy-done.5, s32[1,8]{1,0:T(1,128)S(1)} %copy-done.6, f32[2,8,256,256]{3,2,1,0:T(8,128)} %bitcast.5, ...), custom_call_target="tpu_custom_call" | custom-call | tf_op jit(solution)/shard_map/slots/pallas_call | solution.py:313
  73.6 5.2 %deposit.1 = f32[2,2048,256]{2,1,0:T(8,128)} custom-call(s32[64]{0:T(128)S(1)} %get-tuple-element.8.index, bf16[6,2,256,256]{3,2,1,0:T(8,128)(2,1)S(1)} %get-tuple-element.9.own_ref, bf16[6,2,256,256]{3,2,1,0:T(8,128)(2,1)S(1)} %get-tuple-element.10.halo_ref), custom_call_target="tpu_custom_call" | custom-call | tf_op jit(solution)/shard_map/deposit/pallas_call | solution.py:363
Async XLA Ops:
  0.7 1.0 %copy-start = (f32[2,256,256]{2,1,0:T(8,128)S(1)}, f32[2,256,256]{2,1,0:T(8,128)}, u32[]{:S(2)}) copy-start(f32[2,256,256]{2,1,0:T(8,128)} %probe_hbm.1) | copy-start | bytes 1572868
  1.7 1.0 %copy-start.1 = (bf16[512,512]{1,0:T(8,128)(2,1)S(1)}, bf16[512,512]{1,0:T(8,128)(2,1)}, u32[]{:S(2)}) copy-start(bf16[512,512]{1,0:T(8,128)(2,1)} %constant.5.clone.inv_hbm) | copy-start | bytes 1572868
  2.7 1.0 %copy-start.2 = (bf16[512,512]{1,0:T(8,128)(2,1)S(1)}, bf16[512,512]{1,0:T(8,128)(2,1)}, u32[]{:S(2)}) copy-start(bf16[512,512]{1,0:T(8,128)(2,1)} %constant.4.clone.fwd_hbm) | copy-start | bytes 1572868
  3.8 0.9 %copy-start.3 = (f32[1,256,256]{2,1,0:T(8,128)S(1)}, f32[1,256,256]{2,1,0:T(8,128)}, u32[]{:S(2)}) copy-start(f32[1,256,256]{2,1,0:T(8,128)} %param.12) | copy-start | bytes 786436
  4.7 0.7 copy-start.4
  5.4 0.7 copy-start.5
  6.0 0.7 copy-start.6

commit v2 on v1

v2 whole, which is shorter than its diff:
```python
import jax
import jax.numpy as jnp
import numpy as np
from jax import lax
from jax.experimental import pallas as pl
from jax.experimental.pallas import tpu as pltpu
from jax.sharding import PartitionSpec as P

BF16 = jnp.bfloat16
F32 = jnp.float32


def dft_tables(length):
    index = np.arange(length, dtype=np.int32)
    product = index[:, None] * index[None, :] % length
    angle = product.astype(np.float32) * np.float32(2.0 * np.pi / length)
    scale = np.float32(length ** (-0.5))
    cosine = np.cos(angle) * scale
    sine = np.sin(angle) * scale
    forward = np.block([[cosine, -sine], [sine, cosine]])
    inverse = np.block([[cosine, sine], [-sine, cosine]])
    return forward.astype(BF16), inverse.astype(BF16)


def iota(shape, axis):
    return lax.broadcasted_iota(jnp.int32, shape, axis)


def slot_of(item, cut):
    return 2 * jnp.where(item == 0, 0, jnp.where(item == 2, 1, 2)) + cut


def slot_kernel(
    counts_hbm, chosen_hbm, row_hbm, column_hbm,
    obj_hbm, probe_hbm, phase_hbm, intensity_hbm, fwd_hbm, inv_hbm,
    index_out, out,
    obj, probe, phase, trig, intensity, fwd, inv,
    own, own_send, far, send_left, send_right, level_send, level_far, measured,
    terms, psi0, psi1, window, xbuf, ybuf,
    index, counts, chosen, row_offset, column_offset,
    in_sem, index_sem, phase_sem, level_sem, own_ssem, own_rsem, left_ssem, right_ssem, far_rsem,
    keep_sem, part_ssem, part_rsem, edge_ssem, edge_rsem,
):
    slots = chosen.shape[1]
    size = probe.shape[-1]
    items = terms.shape[0]
    last_block = obj.shape[1] - 1
    core = lax.axis_index("cuts")
    tile = lax.axis_index("tile")
    tiles = lax.axis_size("tile")
    other = 1 - core
    right = lax.rem(tile + 1, tiles)
    left = lax.rem(tile + tiles - 1, tiles)
    has_left = tile > 0
    has_right = tile < tiles - 1
    partner = {"cuts": other, "tile": tile}

    def copy_in(source, target, number):
        return pltpu.make_async_copy(source, target, in_sem.at[number])

    scalars = [
        copy_in(counts_hbm, counts, 0),
        copy_in(chosen_hbm, chosen, 1),
        copy_in(row_hbm, row_offset, 2),
        copy_in(column_hbm, column_offset, 3),
    ]
    load_obj = copy_in(obj_hbm, obj, 4)
    load_phase = copy_in(phase_hbm, phase.at[core], 5)
    load_intensity = copy_in(intensity_hbm, intensity, 6)
    rest = [copy_in(probe_hbm, probe, 7), copy_in(fwd_hbm, fwd, 8), copy_in(inv_hbm, inv, 9)]
    for load in scalars + [load_obj, load_phase, load_intensity] + rest:
        load.start()

    for k in range(32):
        index[0, k] = 0

    @pl.when(tile == 0)
    def _():
        for k in range(32):
            index[1, k] = 0

    barrier = pltpu.get_barrier_semaphore()
    pl.semaphore_signal(barrier, inc=1, device_id=partner)
    for there, reached in ((left, has_left), (right, has_right)):

        @pl.when(reached)
        def _(there=there):
            for cut in (0, 1):
                pl.semaphore_signal(barrier, inc=1, device_id={"cuts": cut, "tile": there})

    for load in scalars:
        load.wait()
    for j in range(slots):
        q = chosen[0, j]
        index[0, j] = row_offset[0, q]
        index[0, 8 + j] = column_offset[0, q]
        index[0, 16 + j] = (j < counts[0]).astype(jnp.int32)

    rows = iota((size, size), 0)
    lanes = iota((size, size), 1)

    def fold(row, plane):
        block = lax.shift_right_logical(row, 8)
        after = jnp.minimum(block + 1, last_block)
        here = obj[plane, block]
        below = obj[plane, after]
        return jnp.where(rows >= jnp.bitwise_and(row, size - 1), here, below).astype(BF16)

    index_copy = pltpu.make_async_remote_copy(
        index.at[0], index.at[1], index_sem.at[0], index_sem.at[1],
        device_id={"cuts": core, "tile": right},
    )
    phase_copy = pltpu.make_async_remote_copy(
        phase.at[core], phase.at[core], phase_sem.at[0], phase_sem.at[1], device_id=partner
    )
    level_copy = pltpu.make_async_remote_copy(
        level_send, level_far, level_sem.at[0], level_sem.at[1],
        device_id={"cuts": core, "tile": right},
    )

    def right_copy(half):
        return pltpu.make_async_remote_copy(
            send_right.at[half], far.at[1, core], right_ssem.at[half], far_rsem.at[1, core],
            device_id={"cuts": half, "tile": right},
        )

    def left_copy(j):
        item = 2 * (j // 2)
        return pltpu.make_async_remote_copy(
            send_left.at[j], far.at[item, core], left_ssem.at[j], far_rsem.at[item, core],
            device_id={"cuts": j % 2, "tile": left},
        )

    def own_copy(item):
        return pltpu.make_async_remote_copy(
            own_send.at[item], own.at[item, core], own_ssem.at[item], own_rsem.at[item],
            device_id=partner,
        )

    def near_windows(item):
        flip = int(item == 1)
        row = index[flip, slot_of(item, other)]
        for plane in (0, 1):
            own_send[item, plane] = fold(row, plane)
        own_copy(item).start()
        row = index[flip, slot_of(item, core)]
        for plane in (0, 1):
            own[item, core, plane] = fold(row, plane)

    load_obj.wait()
    for half in (0, 1):
        for plane in (0, 1):
            send_right[half, plane] = fold(index[0, slots - 2 + half], plane)

    peers = 1 + 2 * has_left.astype(jnp.int32) + 2 * has_right.astype(jnp.int32)
    pl.semaphore_wait(barrier, peers)

    @pl.when(has_right)
    def _():
        index_copy.start()
        right_copy(0).start()
        right_copy(1).start()

    load_phase.wait()
    phase_copy.start()
    near_windows(0)

    @pl.when(has_left)
    def _():
        index_copy.wait_recv()
        for j in range(slots - 2):
            for plane in (0, 1):
                send_left[j, plane] = fold(index[1, j], plane)
            left_copy(j).start()

    load_intensity.wait()

    @pl.when(has_right)
    def _():
        level_send[...] = intensity[chosen[0, slots - 2 + core]].astype(BF16)
        level_copy.start()

    near_windows(2)

    @pl.when(has_left)
    def _():
        near_windows(1)

    @pl.when(jnp.logical_not(has_right))
    def _():
        near_windows(3)

    for k in range(32):
        index_out[k] = index[0, k]
        index_out[32 + k] = index[1, k]

    phase_copy.wait_recv()

    @pl.loop(0, 2 * size // 32)
    def _(k):
        cut = k // (size // 32)
        start = pl.multiple_of(lax.rem(k, size // 32) * 32, 32)
        angle = phase[cut, pl.ds(start, 32), :]
        trig[cut, 0, pl.ds(start, 32), :] = jnp.cos(angle)
        trig[cut, 1, pl.ds(start, 32), :] = jnp.sin(angle)

    for load in rest:
        load.wait()

    def stage(real, imag):
        xbuf[:, :size] = real.astype(BF16)
        xbuf[:, size:] = imag.astype(BF16)

    def transform(right_table, left_table):
        halfway = jnp.dot(xbuf[...], right_table[...], preferred_element_type=F32)
        ybuf[:size, :] = halfway[:, :size].astype(BF16)
        ybuf[size:, :] = halfway[:, size:].astype(BF16)
        field = jnp.dot(left_table[...], ybuf[...], preferred_element_type=F32)
        return field[:size], field[size:]

    def propagate(real, imag, cut, sign):
        stage(real, imag)
        real, imag = transform(fwd, inv)
        cosine = trig[cut, 0]
        sine = trig[cut, 1] * sign
        stage(real * cosine - imag * sine, real * sine + imag * cosine)
        return transform(inv, fwd)

    def kind(item):
        return (item == 1).astype(jnp.int32)

    def exists(item):
        return jnp.where(item == 1, has_left, jnp.where(item == 3, jnp.logical_not(has_right), True))

    def has_far(item):
        return jnp.where(item == 1, has_left, has_right)

    def edge_copy(item, cut):
        flip = kind(item)
        j = slot_of(item, core)
        return pltpu.make_async_remote_copy(
            terms.at[item, cut], out.at[1 - flip, j], edge_ssem.at[item, cut], edge_rsem.at[1 - flip, j],
            device_id={"cuts": cut, "tile": jnp.where(flip == 1, left, right)},
        )

    def part_copy(item):
        return pltpu.make_async_remote_copy(
            terms.at[item, other], out.at[kind(item), slot_of(item, core)],
            part_ssem.at[item], part_rsem.at[item], device_id=partner,
        )

    def keep_copy(item):
        return pltpu.make_async_copy(
            terms.at[item, core], out.at[kind(item), slot_of(item, core)], keep_sem.at[item]
        )

    def work(item):
        flip = kind(item)
        j = slot_of(item, core)
        row = jnp.bitwise_and(index[flip, j], size - 1)
        column = index[flip, 8 + j]
        live = index[flip, 16 + j] > 0
        to_row = (rows == jnp.bitwise_and(lanes + row, size - 1)).astype(F32).astype(BF16)
        to_lane = (lanes == jnp.bitwise_and(rows + column, size - 1)).astype(F32).astype(BF16)

        def moved(value):
            moving = jnp.dot(value, to_lane, preferred_element_type=F32).astype(BF16)
            return jnp.dot(to_row, moving, preferred_element_type=F32)

        def shifted(value):
            high = value.astype(BF16)
            low = (value - high.astype(F32)).astype(BF16)
            return moved(high) + moved(low)

        for plane in (0, 1):
            psi0[plane] = shifted(probe[plane])
        own_copy(item).wait_recv()
        start = jnp.where(flip == 1, 0, column)
        stop = jnp.where(flip == 1, column, size)
        inside = (lanes >= start) & (lanes < stop)

        @pl.when(has_far(item))
        def _():
            for cut in (0, 1):
                pltpu.make_async_remote_copy(
                    send_left.at[0], far.at[item, cut], left_ssem.at[0], far_rsem.at[item, cut],
                    device_id={"cuts": cut, "tile": right},
                ).wait_recv()
                for plane in (0, 1):
                    window[cut, plane] = jnp.where(
                        inside, own[item, cut, plane].astype(F32), far[item, cut, plane].astype(F32)
                    )

        @pl.when(jnp.logical_not(has_far(item)))
        def _():
            for cut in (0, 1):
                for plane in (0, 1):
                    window[cut, plane] = jnp.where(inside, own[item, cut, plane].astype(F32), 0.0)

        @pl.when(flip == 1)
        def _():
            level_copy.wait_recv()
            measured[...] = level_far[...].astype(F32)

        @pl.when(flip == 0)
        def _():
            measured[...] = intensity[chosen[0, j]]

        real, imag = psi0[0], psi0[1]
        o_real, o_imag = window[0, 0], window[0, 1]
        real, imag = propagate(real * o_real - imag * o_imag, real * o_imag + imag * o_real, 0, 1.0)
        psi1[0] = real.astype(BF16)
        psi1[1] = imag.astype(BF16)
        real, imag = psi1[0].astype(F32), psi1[1].astype(F32)
        o_real, o_imag = window[1, 0], window[1, 1]
        real, imag = propagate(real * o_real - imag * o_imag, real * o_imag + imag * o_real, 1, 1.0)
        real, imag = real.astype(BF16).astype(F32), imag.astype(BF16).astype(F32)
        factor = 2.0 * (real * real + imag * imag - shifted(measured[...]))
        real = jnp.where(live, factor * real, 0.0)
        imag = jnp.where(live, factor * imag, 0.0)

        def emit(cut, wave, real, imag):
            w_real, w_imag = wave[0].astype(F32), wave[1].astype(F32)
            terms[item, cut, 0] = (w_real * real + w_imag * imag).astype(BF16)
            terms[item, cut, 1] = (w_real * imag - w_imag * real).astype(BF16)

            @pl.when(has_far(item))
            def _():
                edge_copy(item, cut).start()

        real, imag = propagate(real, imag, 1, -1.0)
        emit(1, psi1, real, imag)
        o_real, o_imag = window[1, 0], window[1, 1]
        real, imag = propagate(
            o_real * real + o_imag * imag, o_real * imag - o_imag * real, 0, -1.0
        )
        emit(0, psi0, real, imag)
        part_copy(item).start()
        keep_copy(item).start()

    @pl.loop(0, items)
    def _(item):
        @pl.when(exists(item))
        def _():
            work(item)

    phase_copy.wait_send()

    @pl.loop(0, items)
    def _(item):
        @pl.when(exists(item))
        def _():
            own_copy(item).wait_send()
            keep_copy(item).wait()
            part_copy(item).wait_send()
            part_copy(item).wait_recv()

            @pl.when(has_far(item))
            def _():
                edge_copy(item, 0).wait_send()
                edge_copy(item, 1).wait_send()

    def edge_arrives(kept, j):
        pltpu.make_async_remote_copy(
            terms.at[0, 0], out.at[kept, j], edge_ssem.at[0, 0], edge_rsem.at[kept, j],
            device_id={"cuts": core, "tile": right},
        ).wait_recv()

    @pl.when(has_right)
    def _():
        index_copy.wait_send()
        level_copy.wait_send()
        for half in (0, 1):
            right_copy(half).wait_send()
            edge_arrives(0, slots - 2 + half)

    @pl.when(has_left)
    def _():
        for j in range(slots - 2):
            left_copy(j).wait_send()
            edge_arrives(1, j)


def deposit_kernel(index, terms_ref, out_ref):
    block = pl.program_id(0)
    slots = terms_ref.shape[1]
    size = out_ref.shape[-1]
    rows = iota((size, size), 0)
    lanes = iota((size, size), 1)
    has_left = lax.axis_index("tile") > 0
    out_ref[...] = jnp.zeros_like(out_ref)

    for base in (0, 32):

        @pl.loop(0, slots)
        def _(j, base=base):
            row = index[base + j]
            column = index[base + 8 + j]
            first = lax.shift_right_logical(row, 8)
            start = jnp.bitwise_and(row, size - 1)
            live = index[base + 16 + j] > 0
            if base:
                live = live & has_left

            @pl.when(live & ((first == block) | (first + 1 == block)))
            def _():
                above = first == block
                low = jnp.where(above, start, 0)
                high = jnp.where(above, size, start)
                mask = (rows >= low) & (rows < high)
                mask = mask & ((lanes < column) if base else (lanes >= column))
                for plane in (0, 1):
                    out_ref[plane] += jnp.where(mask, terms_ref[base // 32, j, plane].astype(F32), 0.0)


def on_device(
    object_slices, probe_field, slice_phase, intensity, counts, chosen, row_offset, column_offset
):
    _, _, height, breadth = object_slices.shape
    size = probe_field.shape[-1]
    scan = row_offset.shape[1]
    slots = chosen.shape[1]
    items = 4
    forward, inverse = dft_tables(size)
    smem = pl.BlockSpec(memory_space=pltpu.SMEM)
    anywhere = pl.BlockSpec(memory_space=pl.ANY)
    stay = pl.BlockSpec(memory_space=pltpu.HBM)
    plane = (size, size)
    dma = pltpu.SemaphoreType.DMA
    operands = (
        chosen, row_offset, column_offset,
        object_slices.reshape(2, height // size, size, breadth), probe_field, slice_phase[0],
        intensity[0], jnp.asarray(forward), jnp.asarray(inverse),
    )
    index, terms = pl.pallas_call(
        slot_kernel,
        out_shape=(
            jax.ShapeDtypeStruct((64,), jnp.int32),
            jax.ShapeDtypeStruct((2, slots, 2) + plane, BF16),
        ),
        in_specs=[stay] * 10,
        out_specs=(smem, anywhere),
        scratch_shapes=[
            pltpu.VMEM((2, height // size) + plane, F32),
            pltpu.VMEM((2,) + plane, F32),
            pltpu.VMEM((2,) + plane, F32),
            pltpu.VMEM((2, 2) + plane, F32),
            pltpu.VMEM((scan,) + plane, F32),
            pltpu.VMEM((2 * size, 2 * size), BF16),
            pltpu.VMEM((2 * size, 2 * size), BF16),
            pltpu.VMEM((items, 2, 2) + plane, BF16),
            pltpu.VMEM((items, 2) + plane, BF16),
            pltpu.VMEM((items, 2, 2) + plane, BF16),
            pltpu.VMEM((slots - 2, 2) + plane, BF16),
            pltpu.VMEM((2, 2) + plane, BF16),
            pltpu.VMEM(plane, BF16),
            pltpu.VMEM(plane, BF16),
            pltpu.VMEM(plane, F32),
            pltpu.VMEM((items, 2, 2) + plane, BF16),
            pltpu.VMEM((2,) + plane, F32),
            pltpu.VMEM((2,) + plane, BF16),
            pltpu.VMEM((2, 2) + plane, F32),
            pltpu.VMEM((size, 2 * size), BF16),
            pltpu.VMEM((2 * size, size), BF16),
            pltpu.SMEM((2, 32), jnp.int32),
            pltpu.SMEM((1,), jnp.int32),
            pltpu.SMEM((1, slots), jnp.int32),
            pltpu.SMEM((1, scan), jnp.int32),
            pltpu.SMEM((1, scan), jnp.int32),
            dma((10,)),
            dma((2,)),
            dma((2,)),
            dma((2,)),
            dma((items,)),
            dma((items,)),
            dma((slots - 2,)),
            dma((2,)),
            dma((items, 2)),
            dma((items,)),
            dma((items,)),
            dma((items,)),
            dma((items, 2)),
            dma((2, slots)),
        ],
        compiler_params=pltpu.CompilerParams(
            collective_id=0, has_side_effects=True, vmem_limit_bytes=48 * 1024 * 1024
        ),
        name="slots",
    )(counts, *[pltpu.with_memory_space_constraint(operand, pltpu.HBM) for operand in operands])
    gradient = pl.pallas_call(
        deposit_kernel,
        grid_spec=pltpu.PrefetchScalarGridSpec(
            num_scalar_prefetch=1,
            grid=(height // size,),
            in_specs=[
                pl.BlockSpec(
                    (2, slots, 2) + plane,
                    lambda b, *_: (0, 0, 0, 0, 0),
                    pipeline_mode=pl.Buffered(1),
                )
            ],
            out_specs=pl.BlockSpec((2, size, breadth), lambda b, *_: (0, b, 0)),
        ),
        out_shape=jax.ShapeDtypeStruct((2, height, breadth), F32),
        compiler_params=pltpu.CompilerParams(vmem_limit_bytes=32 * 1024 * 1024),
        name="deposit",
    )(index, terms)
    return gradient[None]


def solution(mesh):
    return jax.shard_map(
        on_device,
        mesh=mesh,
        in_specs=(
            P("cuts", None, None, "tile"),
            P(),
            P("cuts", None, None),
            P("tile", None, None, None),
            P("tile"),
            P("tile", None),
            P("tile", None),
            P("tile", None),
        ),
        out_specs=P("cuts", None, None, "tile"),
        check_vma=False,
    )
```

time: 79.1 us -> 60.1 us (0.76)
  the two profiles are of different devices: /device:TPU:0 before, /device:TPU:160 now
where the time goes in v2:
time: 60.1 us; the launch traced here: 59.1 us
  Pallas kernels  58.4 us (97%)
  between operations  0.66 us (1%)
    pallas_call x1, Pallas kernels, on_device(): pl.pallas_call(slot_kernel, out_shape=(jax.ShapeDtypeStruct((64,), jnp.in...  53 us
    pallas_call x1, Pallas kernels, on_device(): pl.pallas_call(deposit_kernel, grid_spec=pltpu.PrefetchScalarGridSpec(num...  5.42 us

profile of v2, /device:TPU:160, one launch (start us, length us, event | category | flops | bytes accessed | tf_op | source)
XLA Modules:
  0.0 59.1 jit_solution(816906074102409928)
XLA Ops:
  0.7 53.0 %slots.1 = (s32[64]{0:T(128)S(1)}, bf16[2,6,2,256,256]{4,3,2,1,0:T(8,128)(2,1)S(1)}) custom-call(s32[1]{0:T(128)S(6)} %copy.11.counts_hbm, s32[1,6]{1,0:T(1,128)} %chosen_hbm.1, s32[1,8]{1,0:T(1,128)} %row_hbm.1, s32[1,8]{1,0:T(1,128)} %column_hbm.1, f32[2,8,256,256]{3,2,1,0:T(8,128)} %bitcast.4, f32[2,256,256]{2,1,0:T(8,128)} %probe_hbm.1, ...), custom_call_target="tpu_custom_call" | custom-call | tf_op jit(solution)/shard_map/slots/pallas_call | solution.py:435
  53.7 5.4 %deposit.1 = f32[2,2048,256]{2,1,0:T(8,128)} custom-call(s32[64]{0:T(128)S(1)} %get-tuple-element.7.index, bf16[2,6,2,256,256]{4,3,2,1,0:T(8,128)(2,1)S(1)} %get-tuple-element.8.terms_ref), custom_call_target="tpu_custom_call" | custom-call | tf_op jit(solution)/shard_map/deposit/pallas_call | solution.py:490

commit v3 on v2

--- a/solution.py
+++ b/solution.py
@@ -27,7 +27,7 @@
 
 
 def slot_of(item, cut):
-    return 2 * jnp.where(item == 0, 0, jnp.where(item == 2, 1, 2)) + cut
+    return lax.rem(3 * cut + 4 * item, 6)
 
 
 def slot_kernel(
@@ -38,10 +38,11 @@
     own, own_send, far, send_left, send_right, level_send, level_far, measured,
     terms, psi0, psi1, window, xbuf, ybuf,
     index, counts, chosen, row_offset, column_offset,
-    in_sem, index_sem, phase_sem, level_sem, own_ssem, own_rsem, left_ssem, right_ssem, far_rsem,
+    in_sem, index_sem, phase_sem, level_ssem, level_rsem, own_ssem, own_rsem, left_ssem, right_ssem, far_rsem,
     keep_sem, part_ssem, part_rsem, edge_ssem, edge_rsem,
 ):
     slots = chosen.shape[1]
+    kept = slots // 2
     size = probe.shape[-1]
     items = terms.shape[0]
     last_block = obj.shape[1] - 1
@@ -113,21 +114,22 @@
     phase_copy = pltpu.make_async_remote_copy(
         phase.at[core], phase.at[core], phase_sem.at[0], phase_sem.at[1], device_id=partner
     )
-    level_copy = pltpu.make_async_remote_copy(
-        level_send, level_far, level_sem.at[0], level_sem.at[1],
-        device_id={"cuts": core, "tile": right},
-    )
-
-    def right_copy(half):
+    def level_copy(n):
         return pltpu.make_async_remote_copy(
-            send_right.at[half], far.at[1, core], right_ssem.at[half], far_rsem.at[1, core],
-            device_id={"cuts": half, "tile": right},
+            level_send.at[n], level_far.at[n], level_ssem.at[n], level_rsem.at[n],
+            device_id={"cuts": core, "tile": right},
+        )
+
+    def right_copy(j):
+        return pltpu.make_async_remote_copy(
+            send_right.at[j - kept], far.at[j // 2, core],
+            right_ssem.at[j - kept], far_rsem.at[j // 2, core],
+            device_id={"cuts": j % 2, "tile": right},
         )
 
     def left_copy(j):
-        item = 2 * (j // 2)
         return pltpu.make_async_remote_copy(
-            send_left.at[j], far.at[item, core], left_ssem.at[j], far_rsem.at[item, core],
+            send_left.at[j], far.at[j // 2, core], left_ssem.at[j], far_rsem.at[j // 2, core],
             device_id={"cuts": j % 2, "tile": left},
         )
 
@@ -137,58 +139,87 @@
             device_id=partner,
         )
 
-    def near_windows(item):
-        flip = int(item == 1)
-        row = index[flip, slot_of(item, other)]
+    def kind(item, cut):
+        return ((item < 3) & (slot_of(item, cut) >= kept)).astype(jnp.int32)
+
+    def exists(item, cut):
+        away = slot_of(item, cut) >= kept
+        usual = (item < 3) & (jnp.logical_not(away) | has_left)
+        return usual | ((item >= 3) & away & jnp.logical_not(has_right))
+
+    def has_far(item, cut):
+        return jnp.where(kind(item, cut) == 1, has_left, has_right)
+
+    def near_windows(first, last, flip):
+        @pl.loop(first, last)
+        def _(item):
+            @pl.when(exists(item, other) & (kind(item, other) == flip))
+            def _():
+                row = index[flip, slot_of(item, other)]
+                for plane in (0, 1):
+                    own_send[item, plane] = fold(row, plane)
+                own_copy(item).start()
+
+            @pl.when(exists(item, core) & (kind(item, core) == flip))
+            def _():
+                row = index[flip, slot_of(item, core)]
+                for plane in (0, 1):
+                    own[item, core, plane] = fold(row, plane)
+
+    peers = 1 + 2 * has_left.astype(jnp.int32) + 2 * has_right.astype(jnp.int32)
+    load_obj.wait()
+    for plane in (0, 1):
+        send_right[0, plane] = fold(index[0, kept], plane)
+    load_intensity.wait()
+    level_send[0] = intensity[chosen[0, 4 - core]].astype(BF16)
+    level_send[1] = intensity[chosen[0, 5]].astype(BF16)
+    pl.semaphore_wait(barrier, peers)
+
+    @pl.when(has_right)
+    def _():
+        index_copy.start()
+
+        @pl.when(core == 1)
+        def _():
+            level_copy(0).start()
+
+        right_copy(kept).start()
+
+        @pl.when(core == 0)
+        def _():
+            level_copy(0).start()
+
         for plane in (0, 1):
-            own_send[item, plane] = fold(row, plane)
-        own_copy(item).start()
-        row = index[flip, slot_of(item, core)]
+            send_right[1, plane] = fold(index[0, kept + 1], plane)
+        right_copy(kept + 1).start()
+
+        @pl.when(core == 1)
+        def _():
+            level_copy(1).start()
+
         for plane in (0, 1):
-            own[item, core, plane] = fold(row, plane)
-
-    load_obj.wait()
-    for half in (0, 1):
-        for plane in (0, 1):
-            send_right[half, plane] = fold(index[0, slots - 2 + half], plane)
-
-    peers = 1 + 2 * has_left.astype(jnp.int32) + 2 * has_right.astype(jnp.int32)
-    pl.semaphore_wait(barrier, peers)
-
-    @pl.when(has_right)
-    def _():
-        index_copy.start()
-        right_copy(0).start()
-        right_copy(1).start()
+            send_right[2, plane] = fold(index[0, kept + 2], plane)
+        right_copy(kept + 2).start()
 
     load_phase.wait()
     phase_copy.start()
-    near_windows(0)
+    near_windows(0, 3, 0)
 
     @pl.when(has_left)
     def _():
         index_copy.wait_recv()
-        for j in range(slots - 2):
+        for j in range(kept):
             for plane in (0, 1):
                 send_left[j, plane] = fold(index[1, j], plane)
             left_copy(j).start()
 
-    load_intensity.wait()
-
-    @pl.when(has_right)
-    def _():
-        level_send[...] = intensity[chosen[0, slots - 2 + core]].astype(BF16)
-        level_copy.start()
-
-    near_windows(2)
-
     @pl.when(has_left)
     def _():
-        near_windows(1)
+        near_windows(0, 3, 1)
 
     @pl.when(jnp.logical_not(has_right))
     def _():
-        near_windows(3)
+        near_windows(3, items, 0)
 
     for k in range(32):
         index_out[k] = index[0, k]
@@ -226,17 +257,8 @@
         stage(real * cosine - imag * sine, real * sine + imag * cosine)
         return transform(inv, fwd)
 
-    def kind(item):
-        return (item == 1).astype(jnp.int32)
-
-    def exists(item):
-        return jnp.where(item == 1, has_left, jnp.where(item == 3, jnp.logical_not(has_right), True))
-
-    def has_far(item):
-        return jnp.where(item == 1, has_left, has_right)
-
     def edge_copy(item, cut):
-        flip = kind(item)
+        flip = kind(item, core)
         j = slot_of(item, core)
         return pltpu.make_async_remote_copy(
             terms.at[item, cut], out.at[1 - flip, j], edge_ssem.at[item, cut], edge_rsem.at[1 - flip, j],
@@ -245,17 +267,17 @@
 
     def part_copy(item):
         return pltpu.make_async_remote_copy(
-            terms.at[item, other], out.at[kind(item), slot_of(item, core)],
+            terms.at[item, other], out.at[kind(item, core), slot_of(item, core)],
             part_ssem.at[item], part_rsem.at[item], device_id=partner,
         )
 
     def keep_copy(item):
         return pltpu.make_async_copy(
-            terms.at[item, core], out.at[kind(item), slot_of(item, core)], keep_sem.at[item]
+            terms.at[item, core], out.at[kind(item, core), slot_of(item, core)], keep_sem.at[item]
         )
 
     def work(item):
-        flip = kind(item)
+        flip = kind(item, core)
         j = slot_of(item, core)
         row = jnp.bitwise_and(index[flip, j], size - 1)
         column = index[flip, 8 + j]
@@ -279,19 +301,19 @@
         stop = jnp.where(flip == 1, column, size)
         inside = (lanes >= start) & (lanes < stop)
 
-        @pl.when(has_far(item))
+        @pl.when(has_far(item, core))
         def _():
             for cut in (0, 1):
                 pltpu.make_async_remote_copy(
-                    send_left.at[0], far.at[item, cut], left_ssem.at[0], far_rsem.at[item, cut],
+                    send_left.at[0], far.at[j // 2, cut], left_ssem.at[0], far_rsem.at[j // 2, cut],
                     device_id={"cuts": cut, "tile": right},
                 ).wait_recv()
                 for plane in (0, 1):
                     window[cut, plane] = jnp.where(
-                        inside, own[item, cut, plane].astype(F32), far[item, cut, plane].astype(F32)
+                        inside, own[item, cut, plane].astype(F32), far[j // 2, cut, plane].astype(F32)
                     )
 
-        @pl.when(jnp.logical_not(has_far(item)))
+        @pl.when(jnp.logical_not(has_far(item, core)))
         def _():
             for cut in (0, 1):
                 for plane in (0, 1):
@@ -299,8 +321,8 @@
 
         @pl.when(flip == 1)
         def _():
-            level_copy.wait_recv()
-            measured[...] = level_far[...].astype(F32)
+            level_copy(j // 5).wait_recv()
+            measured[...] = level_far[j // 5].astype(F32)
 
         @pl.when(flip == 0)
         def _():
@@ -324,7 +346,7 @@
             terms[item, cut, 0] = (w_real * real + w_imag * imag).astype(BF16)
             terms[item, cut, 1] = (w_real * imag - w_imag * real).astype(BF16)
 
-            @pl.when(has_far(item))
+            @pl.when(has_far(item, core))
             def _():
                 edge_copy(item, cut).start()
 
@@ -339,8 +361,10 @@
         keep_copy(item).start()
 
     @pl.loop(0, items)
-    def _(item):
-        @pl.when(exists(item))
+    def _(turn):
+        item = lax.rem(turn + 3, items)
+
+        @pl.when(exists(item, core))
         def _():
             work(item)
 
@@ -348,17 +372,20 @@
 
     @pl.loop(0, items)
     def _(item):
-        @pl.when(exists(item))
-        def _():
-            own_copy(item).wait_send()
+        @pl.when(exists(item, core))
+        def _():
             keep_copy(item).wait()
             part_copy(item).wait_send()
-            part_copy(item).wait_recv()
-
-            @pl.when(has_far(item))
+
+            @pl.when(has_far(item, core))
             def _():
                 edge_copy(item, 0).wait_send()
                 edge_copy(item, 1).wait_send()
+
+        @pl.when(exists(item, other))
+        def _():
+            own_copy(item).wait_send()
+            part_copy(item).wait_recv()
 
     def edge_arrives(kept, j):
         pltpu.make_async_remote_copy(
@@ -369,48 +396,64 @@
     @pl.when(has_right)
     def _():
         index_copy.wait_send()
-        level_copy.wait_send()
-        for half in (0, 1):
-            right_copy(half).wait_send()
-            edge_arrives(0, slots - 2 + half)
+        level_copy(0).wait_send()
+
+        @pl.when(core == 1)
+        def _():
+            level_copy(1).wait_send()
+
+        for j in range(kept, slots):
+            right_copy(j).wait_send()
+            edge_arrives(0, j)
 
     @pl.when(has_left)
     def _():
-        for j in range(slots - 2):
+        for j in range(kept):
             left_copy(j).wait_send()
             edge_arrives(1, j)
 
 
-def deposit_kernel(index, terms_ref, out_ref):
-    block = pl.program_id(0)
-    slots = terms_ref.shape[1]
-    size = out_ref.shape[-1]
+def deposit_kernel(index, terms, out_hbm, canvas, sem):
+    slots = terms.shape[1]
+    size = canvas.shape[-1]
     rows = iota((size, size), 0)
     lanes = iota((size, size), 1)
     has_left = lax.axis_index("tile") > 0
-    out_ref[...] = jnp.zeros_like(out_ref)
-
-    for base in (0, 32):
-
-        @pl.loop(0, slots)
-        def _(j, base=base):
-            row = index[base + j]
-            column = index[base + 8 + j]
-            first = lax.shift_right_logical(row, 8)
-            start = jnp.bitwise_and(row, size - 1)
-            live = index[base + 16 + j] > 0
-            if base:
-                live = live & has_left
-
-            @pl.when(live & ((first == block) | (first + 1 == block)))
-            def _():
-                above = first == block
-                low = jnp.where(above, start, 0)
-                high = jnp.where(above, size, start)
-                mask = (rows >= low) & (rows < high)
-                mask = mask & ((lanes < column) if base else (lanes >= column))
-                for plane in (0, 1):
-                    out_ref[plane] += jnp.where(mask, terms_ref[base // 32, j, plane].astype(F32), 0.0)
+
+    def write(block):
+        return pltpu.make_async_copy(canvas.at[block], out_hbm.at[:, block], sem.at[block])
+
+    @pl.loop(0, canvas.shape[0])
+    def _(block):
+        canvas[block] = jnp.zeros(canvas.shape[1:], F32)
+        for base in (0, 32):
+
+            @pl.loop(0, slots)
+            def _(j, base=base):
+                row = index[base + j]
+                column = index[base + 8 + j]
+                first = lax.shift_right_logical(row, 8)
+                begin = jnp.bitwise_and(row, size - 1)
+                live = index[base + 16 + j] > 0
+                if base:
+                    live = live & has_left
+
+                @pl.when(live & ((first == block) | (first + 1 == block)))
+                def _():
+                    above = first == block
+                    low = jnp.where(above, begin, 0)
+                    high = jnp.where(above, size, begin)
+                    mask = (rows >= low) & (rows < high)
+                    mask = mask & ((lanes < column) if base else (lanes >= column))
+                    for plane in (0, 1):
+                        added = jnp.where(mask, terms[base // 32, j, plane].astype(F32), 0.0)
+                        canvas[block, plane] = canvas[block, plane] + added
+
+        write(block).start()
+
+    @pl.loop(0, canvas.shape[0])
+    def _(block):
+        write(block).wait()
 
 
 def on_device(
@@ -420,7 +463,7 @@
     size = probe_field.shape[-1]
     scan = row_offset.shape[1]
     slots = chosen.shape[1]
-    items = 4
+    items = slots
     forward, inverse = dft_tables(size)
     smem = pl.BlockSpec(memory_space=pltpu.SMEM)
     anywhere = pl.BlockSpec(memory_space=pl.ANY)
@@ -450,11 +493,11 @@
             pltpu.VMEM((2 * size, 2 * size), BF16),
             pltpu.VMEM((items, 2, 2) + plane, BF16),
             pltpu.VMEM((items, 2) + plane, BF16),
-            pltpu.VMEM((items, 2, 2) + plane, BF16),
-            pltpu.VMEM((slots - 2, 2) + plane, BF16),
-            pltpu.VMEM((2, 2) + plane, BF16),
-            pltpu.VMEM(plane, BF16),
-            pltpu.VMEM(plane, BF16),
+            pltpu.VMEM((3, 2, 2) + plane, BF16),
+            pltpu.VMEM((slots // 2, 2) + plane, BF16),
+            pltpu.VMEM((slots // 2, 2) + plane, BF16),
+            pltpu.VMEM((2,) + plane, BF16),
+            pltpu.VMEM((2,) + plane, BF16),
             pltpu.VMEM(plane, F32),
             pltpu.VMEM((items, 2, 2) + plane, BF16),
             pltpu.VMEM((2,) + plane, F32),
@@ -471,11 +514,12 @@
             dma((2,)),
             dma((2,)),
             dma((2,)),
+            dma((2,)),
             dma((items,)),
             dma((items,)),
-            dma((slots - 2,)),
-            dma((2,)),
-            dma((items, 2)),
+            dma((slots // 2,)),
+            dma((slots // 2,)),
+            dma((3, 2)),
             dma((items,)),
             dma((items,)),
             dma((items,)),
@@ -489,23 +533,17 @@
     )(counts, *[pltpu.with_memory_space_constraint(operand, pltpu.HBM) for operand in operands])
     gradient = pl.pallas_call(
         deposit_kernel,
-        grid_spec=pltpu.PrefetchScalarGridSpec(
-            num_scalar_prefetch=1,
-            grid=(height // size,),
-            in_specs=[
-                pl.BlockSpec(
-                    (2, slots, 2) + plane,
-                    lambda b, *_: (0, 0, 0, 0, 0),
-                    pipeline_mode=pl.Buffered(1),
-                )
-            ],
-            out_specs=pl.BlockSpec((2, size, breadth), lambda b, *_: (0, b, 0)),
-        ),
-        out_shape=jax.ShapeDtypeStruct((2, height, breadth), F32),
+        in_specs=[smem, pl.BlockSpec(memory_space=pltpu.VMEM)],
+        out_specs=anywhere,
+        out_shape=jax.ShapeDtypeStruct((2, height // size, size, breadth), F32),
+        scratch_shapes=[
+            pltpu.VMEM((height // size, 2) + plane, F32),
+            dma((height // size,)),
+        ],
         compiler_params=pltpu.CompilerParams(vmem_limit_bytes=32 * 1024 * 1024),
         name="deposit",
     )(index, terms)
-    return gradient[None]
+    return gradient.reshape(1, 2, height, breadth)
 
 
 def solution(mesh):

time: 60.1 us -> 53.9 us (0.90)
  Pallas kernels: 58.4 us -> 52.7 us
    pallas_call x1, Pallas kernels: 53 us -> 48.7 us  [on_device(): pl.pallas_call(slot_kernel, out_shape=(jax.ShapeDtypeStruct((64,), jnp.in...]
    pallas_call x1, Pallas kernels: 5.42 us -> 3.98 us  [on_device(): pl.pallas_call(deposit_kernel, in_specs=[smem, pl.BlockSpec(memory_space=...]
where the time goes in v3:
time: 53.9 us; the launch traced here: 53.4 us
  Pallas kernels  52.7 us (98%)
  between operations  0.66 us (1%)
    pallas_call x1, Pallas kernels, on_device(): pl.pallas_call(slot_kernel, out_shape=(jax.ShapeDtypeStruct((64,), jnp.in...  48.7 us
    pallas_call x1, Pallas kernels, on_device(): pl.pallas_call(deposit_kernel, in_specs=[smem, pl.BlockSpec(memory_space=...  3.98 us

profile of v3, /device:TPU:160, one launch (start us, length us, event | category | flops | bytes accessed | tf_op | source)
XLA Modules:
  0.0 53.4 jit_solution(1150686851966562462)
XLA Ops:
  0.7 48.7 %slots.1 = (s32[64]{0:T(128)S(1)}, bf16[2,6,2,256,256]{4,3,2,1,0:T(8,128)(2,1)S(1)}) custom-call(s32[1]{0:T(128)S(6)} %copy.11.counts_hbm, s32[1,6]{1,0:T(1,128)} %chosen_hbm.1, s32[1,8]{1,0:T(1,128)} %row_hbm.1, s32[1,8]{1,0:T(1,128)} %column_hbm.1, f32[2,8,256,256]{3,2,1,0:T(8,128)} %bitcast.4, f32[2,256,256]{2,1,0:T(8,128)} %probe_hbm.1, ...), custom_call_target="tpu_custom_call" | custom-call | tf_op jit(solution)/shard_map/slots/pallas_call | solution.py:478
  49.4 4.0 %deposit.1 = f32[2,8,256,256]{3,2,1,0:T(8,128)} custom-call(s32[64]{0:T(128)S(1)} %get-tuple-element.7.index, bf16[2,6,2,256,256]{4,3,2,1,0:T(8,128)(2,1)S(1)} %get-tuple-element.8.terms), custom_call_target="tpu_custom_call" | custom-call | tf_op jit(solution)/shard_map/deposit/pallas_call | solution.py:534

commit v4 on v3

--- a/solution.py
+++ b/solution.py
@@ -69,12 +69,6 @@
     load_phase = copy_in(phase_hbm, phase.at[core], 5)
     load_intensity = copy_in(intensity_hbm, intensity, 6)
     rest = [copy_in(probe_hbm, probe, 7), copy_in(fwd_hbm, fwd, 8), copy_in(inv_hbm, inv, 9)]
-    for load in scalars + [load_obj, load_phase, load_intensity] + rest:
-        load.start()
-
-    for k in range(32):
-        index[0, k] = 0
-
     @pl.when(tile == 0)
     def _():
         for k in range(32):
@@ -89,6 +83,11 @@
             for cut in (0, 1):
                 pl.semaphore_signal(barrier, inc=1, device_id={"cuts": cut, "tile": there})
 
+    for load in scalars + [load_obj, load_phase, load_intensity] + rest:
+        load.start()
+
+    for k in range(32):
+        index[0, k] = 0
     for load in scalars:
         load.wait()
     for j in range(slots):
@@ -221,9 +220,15 @@
     def _():
         near_windows(3, items, 0)
 
-    for k in range(32):
-        index_out[k] = index[0, k]
-        index_out[32 + k] = index[1, k]
+    for base in (0, 1):
+        for j in range(slots):
+            row = index[base, j]
+            live = index[base, 16 + j] > 0
+            index_out[32 * base + j] = jnp.where(live, lax.shift_right_logical(row, 8), -9)
+            index_out[32 * base + 8 + j] = jnp.bitwise_and(row, size - 1)
+            index_out[32 * base + 16 + j] = index[base, 8 + j]
+        for k in (6, 7, 14, 15, 22, 23, 24, 25, 26, 27, 28, 29, 30, 31):
+            index_out[32 * base + k] = 0
 
     phase_copy.wait_recv()
 
@@ -416,9 +421,9 @@
 def deposit_kernel(index, terms, out_hbm, canvas, sem):
     slots = terms.shape[1]
     size = canvas.shape[-1]
-    rows = iota((size, size), 0)
-    lanes = iota((size, size), 1)
-    has_left = lax.axis_index("tile") > 0
+    strip = 32
+    rows = iota((strip, size), 0)
+    lanes = iota((strip, size), 1)
 
     def write(block):
         return pltpu.make_async_copy(canvas.at[block], out_hbm.at[:, block], sem.at[block])
@@ -426,28 +431,26 @@
     @pl.loop(0, canvas.shape[0])
     def _(block):
         canvas[block] = jnp.zeros(canvas.shape[1:], F32)
-        for base in (0, 32):
-
-            @pl.loop(0, slots)
-            def _(j, base=base):
-                row = index[base + j]
-                column = index[base + 8 + j]
-                first = lax.shift_right_logical(row, 8)
-                begin = jnp.bitwise_and(row, size - 1)
-                live = index[base + 16 + j] > 0
-                if base:
-                    live = live & has_left
-
-                @pl.when(live & ((first == block) | (first + 1 == block)))
-                def _():
-                    above = first == block
-                    low = jnp.where(above, begin, 0)
-                    high = jnp.where(above, size, begin)
-                    mask = (rows >= low) & (rows < high)
-                    mask = mask & ((lanes < column) if base else (lanes >= column))
-                    for plane in (0, 1):
-                        added = jnp.where(mask, terms[base // 32, j, plane].astype(F32), 0.0)
-                        canvas[block, plane] = canvas[block, plane] + added
+        for base in (0, 1):
+            for j in range(slots):
+                below = block - index[32 * base + j]
+
+                @pl.when((below == 0) | (below == 1))
+                def _(base=base, j=j, below=below):
+                    begin = index[32 * base + 8 + j]
+                    column = index[32 * base + 16 + j]
+                    low = jnp.where(below == 0, begin, 0)
+                    high = jnp.where(below == 0, size, begin)
+                    columns = (lanes < column) if base else (lanes >= column)
+
+                    @pl.loop(lax.shift_right_logical(low, 5), lax.shift_right_logical(high + strip - 1, 5))
+                    def _(k):
+                        start = pl.multiple_of(k * strip, strip)
+                        mask = columns & (rows >= low - start) & (rows < high - start)
+                        here = pl.ds(start, strip)
+                        for plane in (0, 1):
+                            added = terms[base, j, plane, here, :].astype(F32)
+                            canvas[block, plane, here, :] += jnp.where(mask, added, 0.0)
 
         write(block).start()
 

time: 53.9 us -> 53.1 us (0.985)
  Pallas kernels: 52.7 us -> 51.8 us
    pallas_call x1, Pallas kernels: 3.98 us -> 2.99 us  [on_device(): pl.pallas_call(deposit_kernel, in_specs=[smem, pl.BlockSpec(memory_space=...]
where the time goes in v4:
time: 53.1 us; the launch traced here: 52.4 us
  Pallas kernels  51.8 us (98%)
  between operations  0.66 us (1%)
    pallas_call x1, Pallas kernels, on_device(): pl.pallas_call(slot_kernel, out_shape=(jax.ShapeDtypeStruct((64,), jnp.in...  48.8 us
    pallas_call x1, Pallas kernels, on_device(): pl.pallas_call(deposit_kernel, in_specs=[smem, pl.BlockSpec(memory_space=...  2.99 us

profile of v4, /device:TPU:160, one launch (start us, length us, event | category | flops | bytes accessed | tf_op | source)
XLA Modules:
  0.0 52.4 jit_solution(17127590782029050697)
XLA Ops:
  0.7 48.8 %slots.1 = (s32[64]{0:T(128)S(1)}, bf16[2,6,2,256,256]{4,3,2,1,0:T(8,128)(2,1)S(1)}) custom-call(s32[1]{0:T(128)S(6)} %copy.11.counts_hbm, s32[1,6]{1,0:T(1,128)} %chosen_hbm.1, s32[1,8]{1,0:T(1,128)} %row_hbm.1, s32[1,8]{1,0:T(1,128)} %column_hbm.1, f32[2,8,256,256]{3,2,1,0:T(8,128)} %bitcast.4, f32[2,256,256]{2,1,0:T(8,128)} %probe_hbm.1, ...), custom_call_target="tpu_custom_call" | custom-call | tf_op jit(solution)/shard_map/slots/pallas_call | solution.py:481
  49.5 3.0 %deposit.1 = f32[2,8,256,256]{3,2,1,0:T(8,128)} custom-call(s32[64]{0:T(128)S(1)} %get-tuple-element.7.index, bf16[2,6,2,256,256]{4,3,2,1,0:T(8,128)(2,1)S(1)} %get-tuple-element.8.terms), custom_call_target="tpu_custom_call" | custom-call | tf_op jit(solution)/shard_map/deposit/pallas_call | solution.py:537

commit v5 on v4

--- a/solution.py
+++ b/solution.py
@@ -33,10 +33,10 @@
 def slot_kernel(
     counts_hbm, chosen_hbm, row_hbm, column_hbm,
     obj_hbm, probe_hbm, phase_hbm, intensity_hbm, fwd_hbm, inv_hbm,
-    index_out, out,
+    index_out, canvas, final,
     obj, probe, phase, trig, intensity, fwd, inv,
     own, own_send, far, send_left, send_right, level_send, level_far, measured,
-    terms, psi0, psi1, window, xbuf, ybuf,
+    terms, pieces, psi0, psi1, field_, window, xbuf, ybuf,
     index, counts, chosen, row_offset, column_offset,
     in_sem, index_sem, phase_sem, level_ssem, level_rsem, own_ssem, own_rsem, left_ssem, right_ssem, far_rsem,
     keep_sem, part_ssem, part_rsem, edge_ssem, edge_rsem,
@@ -220,15 +220,16 @@
     def _():
         near_windows(3, items, 0)
 
-    for base in (0, 1):
-        for j in range(slots):
-            row = index[base, j]
-            live = index[base, 16 + j] > 0
-            index_out[32 * base + j] = jnp.where(live, lax.shift_right_logical(row, 8), -9)
-            index_out[32 * base + 8 + j] = jnp.bitwise_and(row, size - 1)
-            index_out[32 * base + 16 + j] = index[base, 8 + j]
-        for k in (6, 7, 14, 15, 22, 23, 24, 25, 26, 27, 28, 29, 30, 31):
-            index_out[32 * base + k] = 0
+    last_live = (index[1, 16 + kept - 1] > 0) & has_left
+    index_out[0] = jnp.where(last_live, lax.shift_right_logical(index[1, kept - 1], 8), -9)
+    index_out[1] = jnp.bitwise_and(index[1, kept - 1], size - 1)
+    index_out[2] = index[1, 8 + kept - 1]
+    for k in range(3, 8):
+        index_out[k] = 0
+
+    @pl.loop(0, canvas.shape[0])
+    def _(block):
+        canvas[block] = jnp.zeros(canvas.shape[1:], F32)
 
     phase_copy.wait_recv()
 
@@ -243,42 +244,76 @@
     for load in rest:
         load.wait()
 
-    def stage(real, imag):
-        xbuf[:, :size] = real.astype(BF16)
-        xbuf[:, size:] = imag.astype(BF16)
-
-    def transform(right_table, left_table):
-        halfway = jnp.dot(xbuf[...], right_table[...], preferred_element_type=F32)
-        ybuf[:size, :] = halfway[:, :size].astype(BF16)
-        ybuf[size:, :] = halfway[:, size:].astype(BF16)
-        field = jnp.dot(left_table[...], ybuf[...], preferred_element_type=F32)
-        return field[:size], field[size:]
-
-    def propagate(real, imag, cut, sign):
-        stage(real, imag)
-        real, imag = transform(fwd, inv)
-        cosine = trig[cut, 0]
-        sine = trig[cut, 1] * sign
-        stage(real * cosine - imag * sine, real * sine + imag * cosine)
-        return transform(inv, fwd)
+    strip = 256
+
+    def transform(right_table, left_table, finish):
+        for start in range(0, size, strip):
+            halfway = jnp.dot(
+                xbuf[start:start + strip, :], right_table[...], preferred_element_type=F32
+            ).astype(BF16)
+            ybuf[start:start + strip, :] = halfway[:, :size]
+            ybuf[size + start:size + start + strip, :] = halfway[:, size:]
+        for start in range(0, size, strip):
+            real = jnp.dot(
+                left_table[start:start + strip, :], ybuf[...], preferred_element_type=F32
+            )
+            imag = jnp.dot(
+                left_table[size + start:size + start + strip, :], ybuf[...], preferred_element_type=F32
+            )
+            finish(slice(start, start + strip), real, imag)
+
+    def put(here, real, imag):
+        xbuf[here, :size] = real.astype(BF16)
+        xbuf[here, size:] = imag.astype(BF16)
+
+    def propagate(field, cut, sign, finish):
+        for start in range(0, size, strip):
+            here = slice(start, start + strip)
+            put(here, *field(here))
+
+        def turn(here, real, imag):
+            cosine = trig[cut, 0, here, :]
+            sine = trig[cut, 1, here, :] * sign
+            put(here, real * cosine - imag * sine, real * sine + imag * cosine)
+
+        transform(fwd, inv, turn)
+        transform(inv, fwd, finish)
 
     def edge_copy(item, cut):
         flip = kind(item, core)
         j = slot_of(item, core)
         return pltpu.make_async_remote_copy(
-            terms.at[item, cut], out.at[1 - flip, j], edge_ssem.at[item, cut], edge_rsem.at[1 - flip, j],
+            terms.at[item, cut], pieces.at[1 - flip, j], edge_ssem.at[item, cut], edge_rsem.at[1 - flip, j],
             device_id={"cuts": cut, "tile": jnp.where(flip == 1, left, right)},
         )
+
+    def final_copy(item, cut):
+        return pltpu.make_async_remote_copy(
+            terms.at[item, cut], final, edge_ssem.at[item, cut], edge_rsem.at[1, kept - 1],
+            device_id={"cuts": cut, "tile": right},
+        )
+
+    def is_final(item):
+        return (item < 3) & (slot_of(item, core) == kept - 1)
+
+    def send_edge(item, cut):
+        @pl.when(has_far(item, core) & is_final(item))
+        def _():
+            final_copy(item, cut).start()
+
+        @pl.when(has_far(item, core) & jnp.logical_not(is_final(item)))
+        def _():
+            edge_copy(item, cut).start()
 
     def part_copy(item):
         return pltpu.make_async_remote_copy(
-            terms.at[item, other], out.at[kind(item, core), slot_of(item, core)],
+            terms.at[item, other], pieces.at[kind(item, core), slot_of(item, core)],
             part_ssem.at[item], part_rsem.at[item], device_id=partner,
         )
 
     def keep_copy(item):
         return pltpu.make_async_copy(
-            terms.at[item, core], out.at[kind(item, core), slot_of(item, core)], keep_sem.at[item]
+            terms.at[item, core], pieces.at[kind(item, core), slot_of(item, core)], keep_sem.at[item]
         )
 
     def work(item):
@@ -333,35 +368,51 @@
         def _():
             measured[...] = intensity[chosen[0, j]]
 
-        real, imag = psi0[0], psi0[1]
-        o_real, o_imag = window[0, 0], window[0, 1]
-        real, imag = propagate(real * o_real - imag * o_imag, real * o_imag + imag * o_real, 0, 1.0)
-        psi1[0] = real.astype(BF16)
-        psi1[1] = imag.astype(BF16)
-        real, imag = psi1[0].astype(F32), psi1[1].astype(F32)
-        o_real, o_imag = window[1, 0], window[1, 1]
-        real, imag = propagate(real * o_real - imag * o_imag, real * o_imag + imag * o_real, 1, 1.0)
-        real, imag = real.astype(BF16).astype(F32), imag.astype(BF16).astype(F32)
-        factor = 2.0 * (real * real + imag * imag - shifted(measured[...]))
-        real = jnp.where(live, factor * real, 0.0)
-        imag = jnp.where(live, factor * imag, 0.0)
-
-        def emit(cut, wave, real, imag):
-            w_real, w_imag = wave[0].astype(F32), wave[1].astype(F32)
-            terms[item, cut, 0] = (w_real * real + w_imag * imag).astype(BF16)
-            terms[item, cut, 1] = (w_real * imag - w_imag * real).astype(BF16)
-
-            @pl.when(has_far(item, core))
-            def _():
-                edge_copy(item, cut).start()
-
-        real, imag = propagate(real, imag, 1, -1.0)
-        emit(1, psi1, real, imag)
-        o_real, o_imag = window[1, 0], window[1, 1]
-        real, imag = propagate(
-            o_real * real + o_imag * imag, o_real * imag - o_imag * real, 0, -1.0
-        )
-        emit(0, psi0, real, imag)
+        measured[...] = shifted(measured[...])
+
+        def enter(wave, cut):
+            def field(here):
+                real, imag = wave[0, here, :].astype(F32), wave[1, here, :].astype(F32)
+                o_real, o_imag = window[cut, 0, here, :], window[cut, 1, here, :]
+                return real * o_real - imag * o_imag, real * o_imag + imag * o_real
+            return field
+
+        def keep(here, real, imag):
+            psi1[0, here, :] = real.astype(BF16)
+            psi1[1, here, :] = imag.astype(BF16)
+
+        propagate(enter(psi0, 0), 0, 1.0, keep)
+
+        def residual(here, real, imag):
+            real, imag = real.astype(BF16).astype(F32), imag.astype(BF16).astype(F32)
+            factor = 2.0 * (real * real + imag * imag - measured[here, :])
+            field_[0, here, :] = jnp.where(live, factor * real, 0.0)
+            field_[1, here, :] = jnp.where(live, factor * imag, 0.0)
+
+        propagate(enter(psi1, 1), 1, 1.0, residual)
+
+        def stored(here):
+            return field_[0, here, :], field_[1, here, :]
+
+        def emit(cut, wave, onward):
+            def finish(here, real, imag):
+                w_real, w_imag = wave[0, here, :].astype(F32), wave[1, here, :].astype(F32)
+                terms[item, cut, 0, here, :] = (w_real * real + w_imag * imag).astype(BF16)
+                terms[item, cut, 1, here, :] = (w_real * imag - w_imag * real).astype(BF16)
+                if onward:
+                    o_real, o_imag = window[cut, 0, here, :], window[cut, 1, here, :]
+                    field_[0, here, :] = o_real * real + o_imag * imag
+                    field_[1, here, :] = o_real * imag - o_imag * real
+            return finish
+
+        propagate(stored, 1, -1.0, emit(1, psi1, True))
+
+        send_edge(item, 1)
+
+        propagate(stored, 0, -1.0, emit(0, psi0, False))
+
+        send_edge(item, 0)
+
         part_copy(item).start()
         keep_copy(item).start()
 
@@ -382,22 +433,69 @@
             keep_copy(item).wait()
             part_copy(item).wait_send()
 
-            @pl.when(has_far(item, core))
-            def _():
-                edge_copy(item, 0).wait_send()
-                edge_copy(item, 1).wait_send()
-
         @pl.when(exists(item, other))
         def _():
             own_copy(item).wait_send()
             part_copy(item).wait_recv()
 
-    def edge_arrives(kept, j):
+    strip = 64
+    strip_rows = iota((strip, size), 0)
+    strip_lanes = iota((strip, size), 1)
+
+    def add_in(base, j):
+        row = index[base, j]
+        first = lax.shift_right_logical(row, 8)
+        begin = jnp.bitwise_and(row, size - 1)
+        column = index[base, 8 + j]
+        columns = (strip_lanes < column) if base else (strip_lanes >= column)
+
+        @pl.loop(0, canvas.shape[0])
+        def _(block):
+            below = block - first
+            low = jnp.where(below == 0, begin, jnp.where(below == 1, 0, size))
+            high = jnp.where(below == 0, size, begin)
+            for start in range(0, size, strip):
+                mask = columns & (strip_rows >= low - start) & (strip_rows < high - start)
+                here = slice(start, start + strip)
+                for plane in (0, 1):
+                    added = pieces[base, j, plane, here, :].astype(F32)
+                    canvas[block, plane, here, :] += jnp.where(mask, added, 0.0)
+
+    def edge_arrives(base, j):
         pltpu.make_async_remote_copy(
-            terms.at[0, 0], out.at[kept, j], edge_ssem.at[0, 0], edge_rsem.at[kept, j],
+            terms.at[0, 0], pieces.at[base, j], edge_ssem.at[0, 0], edge_rsem.at[base, j],
             device_id={"cuts": core, "tile": right},
         ).wait_recv()
 
+    for j in range(kept):
+        add_in(0, j)
+
+    @pl.when(has_left)
+    def _():
+        for j in range(kept, slots):
+            add_in(1, j)
+
+    for j in range(kept):
+
+        @pl.when(has_right)
+        def _(j=j):
+            edge_arrives(0, kept + j)
+
+        add_in(0, kept + j)
+        if j < kept - 1:
+
+            @pl.when(has_left)
+            def _(j=j):
+                edge_arrives(1, j)
+                add_in(1, j)
+
+    @pl.loop(0, 3)
+    def _(item):
+        @pl.when(exists(item, core) & has_far(item, core))
+        def _():
+            for cut in (0, 1):
+                edge_copy(item, cut).wait_send()
+
     @pl.when(has_right)
     def _():
         index_copy.wait_send()
@@ -409,54 +507,44 @@
 
         for j in range(kept, slots):
             right_copy(j).wait_send()
-            edge_arrives(0, j)
 
     @pl.when(has_left)
     def _():
         for j in range(kept):
             left_copy(j).wait_send()
-            edge_arrives(1, j)
-
-
-def deposit_kernel(index, terms, out_hbm, canvas, sem):
-    slots = terms.shape[1]
-    size = canvas.shape[-1]
-    strip = 32
-    rows = iota((strip, size), 0)
-    lanes = iota((strip, size), 1)
-
-    def write(block):
-        return pltpu.make_async_copy(canvas.at[block], out_hbm.at[:, block], sem.at[block])
+        final_copy(0, 0).wait_recv()
+
+
+def deposit_kernel(index_in, canvas, final, out_hbm, summed, index, index_sem, sem):
+    size = final.shape[-1]
+    rows = iota((size, size), 0)
+    lanes = iota((size, size), 1)
+    fetch = pltpu.make_async_copy(index_in, index, index_sem)
+    fetch.start()
+    fetch.wait()
+    first, begin, column = index[0], index[1], index[2]
 
     @pl.loop(0, canvas.shape[0])
     def _(block):
-        canvas[block] = jnp.zeros(canvas.shape[1:], F32)
-        for base in (0, 1):
-            for j in range(slots):
-                below = block - index[32 * base + j]
-
-                @pl.when((below == 0) | (below == 1))
-                def _(base=base, j=j, below=below):
-                    begin = index[32 * base + 8 + j]
-                    column = index[32 * base + 16 + j]
-                    low = jnp.where(below == 0, begin, 0)
-                    high = jnp.where(below == 0, size, begin)
-                    columns = (lanes < column) if base else (lanes >= column)
-
-                    @pl.loop(lax.shift_right_logical(low, 5), lax.shift_right_logical(high + strip - 1, 5))
-                    def _(k):
-                        start = pl.multiple_of(k * strip, strip)
-                        mask = columns & (rows >= low - start) & (rows < high - start)
-                        here = pl.ds(start, strip)
-                        for plane in (0, 1):
-                            added = terms[base, j, plane, here, :].astype(F32)
-                            canvas[block, plane, here, :] += jnp.where(mask, added, 0.0)
-
-        write(block).start()
+        below = block - first
+        touched = (below == 0) | (below == 1)
+
+        @pl.when(jnp.logical_not(touched))
+        def _():
+            pltpu.make_async_copy(canvas.at[block], out_hbm.at[:, block], sem.at[block]).start()
+
+        @pl.when(touched)
+        def _():
+            mask = (rows >= jnp.where(below == 0, begin, 0)) & (lanes < column)
+            mask = mask & (rows < jnp.where(below == 0, size, begin))
+            for plane in (0, 1):
+                added = jnp.where(mask, final[plane].astype(F32), 0.0)
+                summed[below, plane] = canvas[block, plane] + added
+            pltpu.make_async_copy(summed.at[below], out_hbm.at[:, block], sem.at[block]).start()
 
     @pl.loop(0, canvas.shape[0])
     def _(block):
-        write(block).wait()
+        pltpu.make_async_copy(canvas.at[block], out_hbm.at[:, block], sem.at[block]).wait()
 
 
 def on_device(
@@ -478,14 +566,15 @@
         object_slices.reshape(2, height // size, size, breadth), probe_field, slice_phase[0],
         intensity[0], jnp.asarray(forward), jnp.asarray(inverse),
     )
-    index, terms = pl.pallas_call(
+    index, canvas, final = pl.pallas_call(
         slot_kernel,
         out_shape=(
-            jax.ShapeDtypeStruct((64,), jnp.int32),
-            jax.ShapeDtypeStruct((2, slots, 2) + plane, BF16),
+            jax.ShapeDtypeStruct((8,), jnp.int32),
+            jax.ShapeDtypeStruct((height // size, 2) + plane, F32),
+            jax.ShapeDtypeStruct((2,) + plane, BF16),
         ),
         in_specs=[stay] * 10,
-        out_specs=(smem, anywhere),
+        out_specs=(smem, pl.BlockSpec(memory_space=pltpu.VMEM), anywhere),
         scratch_shapes=[
             pltpu.VMEM((2, height // size) + plane, F32),
             pltpu.VMEM((2,) + plane, F32),
@@ -503,8 +592,10 @@
             pltpu.VMEM((2,) + plane, BF16),
             pltpu.VMEM(plane, F32),
             pltpu.VMEM((items, 2, 2) + plane, BF16),
+            pltpu.VMEM((2, slots, 2) + plane, BF16),
             pltpu.VMEM((2,) + plane, F32),
             pltpu.VMEM((2,) + plane, BF16),
+            pltpu.VMEM((2,) + plane, F32),
             pltpu.VMEM((2, 2) + plane, F32),
             pltpu.VMEM((size, 2 * size), BF16),
             pltpu.VMEM((2 * size, size), BF16),
@@ -536,16 +627,18 @@
     )(counts, *[pltpu.with_memory_space_constraint(operand, pltpu.HBM) for operand in operands])
     gradient = pl.pallas_call(
         deposit_kernel,
-        in_specs=[smem, pl.BlockSpec(memory_space=pltpu.VMEM)],
+        in_specs=[anywhere] + [pl.BlockSpec(memory_space=pltpu.VMEM)] * 2,
         out_specs=anywhere,
         out_shape=jax.ShapeDtypeStruct((2, height // size, size, breadth), F32),
         scratch_shapes=[
-            pltpu.VMEM((height // size, 2) + plane, F32),
+            pltpu.VMEM((2, 2) + plane, F32),
+            pltpu.SMEM((8,), jnp.int32),
+            pltpu.SemaphoreType.DMA,
             dma((height // size,)),
         ],
-        compiler_params=pltpu.CompilerParams(vmem_limit_bytes=32 * 1024 * 1024),
+        compiler_params=pltpu.CompilerParams(vmem_limit_bytes=16 * 1024 * 1024),
         name="deposit",
-    )(index, terms)
+    )(index, canvas, final)
     return gradient.reshape(1, 2, height, breadth)
 
 

time: 53.1 us -> 52.2 us (0.983); the launches traced: 52.4 us -> 52.2 us
  no operation moved by 1% of the time
where the time goes in v5:
time: 52.2 us
  Pallas kernels  51.5 us (99%)
  between operations  0.66 us (1%)
    pallas_call x1, Pallas kernels, on_device(): pl.pallas_call(slot_kernel, out_shape=(jax.ShapeDtypeStruct((8,), jnp.int...  48.8 us
    pallas_call x1, Pallas kernels, on_device(): pl.pallas_call(deposit_kernel, in_specs=[anywhere] + [pl.BlockSpec(memory...  2.71 us

profile of v5, /device:TPU:160, one launch (start us, length us, event | category | flops | bytes accessed | tf_op | source)
XLA Modules:
  0.0 52.2 jit_solution(2329350678316447221)
XLA Ops:
  0.7 48.8 %slots.1 = (s32[8]{0:T(128)S(1)}, f32[8,2,256,256]{3,2,1,0:T(8,128)S(1)}, bf16[2,256,256]{2,1,0:T(8,128)(2,1)S(1)}) custom-call(s32[1]{0:T(128)S(6)} %copy.11.counts_hbm, s32[1,6]{1,0:T(1,128)} %chosen_hbm.1, s32[1,8]{1,0:T(1,128)} %row_hbm.1, s32[1,8]{1,0:T(1,128)} %column_hbm.1, f32[2,8,256,256]{3,2,1,0:T(8,128)} %bitcast.4, f32[2,256,256]{2,1,0:T(8,128)} %probe_hbm.1, ...), custom_call_target="tpu_custom_call" | custom-call | tf_op jit(solution)/shard_map/slots/pallas_call | solution.py:569
  49.5 2.7 %deposit.1 = f32[2,8,256,256]{3,2,1,0:T(8,128)} custom-call(s32[8]{0:T(128)S(1)} %get-tuple-element.8.index_in, f32[8,2,256,256]{3,2,1,0:T(8,128)S(1)} %get-tuple-element.9.canvas, bf16[2,256,256]{2,1,0:T(8,128)(2,1)S(1)} %get-tuple-element.10.final), custom_call_target="tpu_custom_call" | custom-call | tf_op jit(solution)/shard_map/deposit/pallas_call | solution.py:628

commit v6 on v5

--- a/solution.py
+++ b/solution.py
@@ -221,11 +221,13 @@
         near_windows(3, items, 0)
 
     last_live = (index[1, 16 + kept - 1] > 0) & has_left
-    index_out[0] = jnp.where(last_live, lax.shift_right_logical(index[1, kept - 1], 8), -9)
-    index_out[1] = jnp.bitwise_and(index[1, kept - 1], size - 1)
-    index_out[2] = index[1, 8 + kept - 1]
-    for k in range(3, 8):
-        index_out[k] = 0
+    placed = (
+        jnp.where(last_live, lax.shift_right_logical(index[1, kept - 1], 8), -9),
+        jnp.bitwise_and(index[1, kept - 1], size - 1),
+        index[1, 8 + kept - 1],
+    )
+    for k in range(3):
+        index_out[k] = jnp.full(index_out.shape[1:], placed[k], jnp.int32).astype(F32)
 
     @pl.loop(0, canvas.shape[0])
     def _(block):
@@ -515,14 +517,11 @@
         final_copy(0, 0).wait_recv()
 
 
-def deposit_kernel(index_in, canvas, final, out_hbm, summed, index, index_sem, sem):
+def deposit_kernel(index_in, canvas, final, out_hbm, summed, sem):
     size = final.shape[-1]
     rows = iota((size, size), 0)
     lanes = iota((size, size), 1)
-    fetch = pltpu.make_async_copy(index_in, index, index_sem)
-    fetch.start()
-    fetch.wait()
-    first, begin, column = index[0], index[1], index[2]
+    first, begin, column = [jnp.max(index_in[k]).astype(jnp.int32) for k in range(3)]
 
     @pl.loop(0, canvas.shape[0])
     def _(block):
@@ -556,7 +555,6 @@
     slots = chosen.shape[1]
     items = slots
     forward, inverse = dft_tables(size)
-    smem = pl.BlockSpec(memory_space=pltpu.SMEM)
     anywhere = pl.BlockSpec(memory_space=pl.ANY)
     stay = pl.BlockSpec(memory_space=pltpu.HBM)
     plane = (size, size)
@@ -569,12 +567,12 @@
     index, canvas, final = pl.pallas_call(
         slot_kernel,
         out_shape=(
-            jax.ShapeDtypeStruct((8,), jnp.int32),
+            jax.ShapeDtypeStruct((3, 8, 128), F32),
             jax.ShapeDtypeStruct((height // size, 2) + plane, F32),
             jax.ShapeDtypeStruct((2,) + plane, BF16),
         ),
         in_specs=[stay] * 10,
-        out_specs=(smem, pl.BlockSpec(memory_space=pltpu.VMEM), anywhere),
+        out_specs=(pl.BlockSpec(memory_space=pltpu.VMEM),) * 2 + (anywhere,),
         scratch_shapes=[
             pltpu.VMEM((2, height // size) + plane, F32),
             pltpu.VMEM((2,) + plane, F32),
@@ -627,13 +625,11 @@
     )(counts, *[pltpu.with_memory_space_constraint(operand, pltpu.HBM) for operand in operands])
     gradient = pl.pallas_call(
         deposit_kernel,
-        in_specs=[anywhere] + [pl.BlockSpec(memory_space=pltpu.VMEM)] * 2,
+        in_specs=[pl.BlockSpec(memory_space=pltpu.VMEM)] * 3,
         out_specs=anywhere,
         out_shape=jax.ShapeDtypeStruct((2, height // size, size, breadth), F32),
         scratch_shapes=[
             pltpu.VMEM((2, 2) + plane, F32),
-            pltpu.SMEM((8,), jnp.int32),
-            pltpu.SemaphoreType.DMA,
             dma((height // size,)),
         ],
         compiler_params=pltpu.CompilerParams(vmem_limit_bytes=16 * 1024 * 1024),

time: 52.2 us -> 51.2 us (0.981)
  Pallas kernels: 51.5 us -> 50.4 us
    pallas_call x2, Pallas kernels: 51.5 us -> 50.4 us  [the longest x1 48.2 us: on_device(): pl.pallas_call(slot_kernel, out_shape=(jax.ShapeDtypeStruct((3, 8, 128),...]
where the time goes in v6:
time: 51.2 us; the launch traced here: 51.1 us
  Pallas kernels  50.4 us (98%)
  between operations  0.66 us (1%)
    pallas_call x1, Pallas kernels, on_device(): pl.pallas_call(slot_kernel, out_shape=(jax.ShapeDtypeStruct((3, 8, 128),...  48.2 us
    pallas_call x1, Pallas kernels, on_device(): pl.pallas_call(deposit_kernel, in_specs=[pl.BlockSpec(memory_space=pltpu....  2.2 us

profile of v6, /device:TPU:160, one launch (start us, length us, event | category | flops | bytes accessed | tf_op | source)
XLA Modules:
  0.0 51.1 jit_solution(13790909060728252965)
XLA Ops:
  0.7 48.2 %slots.1 = (f32[3,8,128]{2,1,0:T(8,128)S(1)}, f32[8,2,256,256]{3,2,1,0:T(8,128)S(1)}, bf16[2,256,256]{2,1,0:T(8,128)(2,1)S(1)}) custom-call(s32[1]{0:T(128)S(6)} %copy.11.counts_hbm, s32[1,6]{1,0:T(1,128)} %chosen_hbm.1, s32[1,8]{1,0:T(1,128)} %row_hbm.1, s32[1,8]{1,0:T(1,128)} %column_hbm.1, f32[2,8,256,256]{3,2,1,0:T(8,128)} %bitcast.4, ...), custom_call_target="tpu_custom_call" | custom-call | tf_op jit(solution)/shard_map/slots/pallas_call | solution.py:567
  48.9 2.2 %deposit.1 = f32[2,8,256,256]{3,2,1,0:T(8,128)} custom-call(f32[3,8,128]{2,1,0:T(8,128)S(1)} %get-tuple-element.8.index_in, f32[8,2,256,256]{3,2,1,0:T(8,128)S(1)} %get-tuple-element.9.canvas, bf16[2,256,256]{2,1,0:T(8,128)(2,1)S(1)} %get-tuple-element.10.final), custom_call_target="tpu_custom_call" | custom-call | tf_op jit(solution)/shard_map/deposit/pallas_call | solution.py:626

commit v7 on v6

--- a/solution.py
+++ b/solution.py
@@ -169,15 +169,18 @@
     load_obj.wait()
     for plane in (0, 1):
         send_right[0, plane] = fold(index[0, kept], plane)
+    pl.semaphore_wait(barrier, peers)
+
+    @pl.when(has_right)
+    def _():
+        index_copy.start()
+
     load_intensity.wait()
     level_send[0] = intensity[chosen[0, 4 - core]].astype(BF16)
     level_send[1] = intensity[chosen[0, 5]].astype(BF16)
-    pl.semaphore_wait(barrier, peers)
 
     @pl.when(has_right)
     def _():
-        index_copy.start()
-
         @pl.when(core == 1)
         def _():
             level_copy(0).start()

time: 51.2 us -> 51.2 us (level)
  no operation moved by 1% of the time
where the time goes in v7:
time: 51.2 us; the launch traced here: 51 us
  Pallas kernels  50.4 us (98%)
  between operations  0.66 us (1%)
    pallas_call x1, Pallas kernels, on_device(): pl.pallas_call(slot_kernel, out_shape=(jax.ShapeDtypeStruct((3, 8, 128),...  48.2 us
    pallas_call x1, Pallas kernels, on_device(): pl.pallas_call(deposit_kernel, in_specs=[pl.BlockSpec(memory_space=pltpu....  2.2 us

profile of v7, /device:TPU:160, one launch (start us, length us, event | category | flops | bytes accessed | tf_op | source)
XLA Modules:
  0.0 51.0 jit_solution(5121170236101256339)
XLA Ops:
  0.7 48.2 %slots.1 = (f32[3,8,128]{2,1,0:T(8,128)S(1)}, f32[8,2,256,256]{3,2,1,0:T(8,128)S(1)}, bf16[2,256,256]{2,1,0:T(8,128)(2,1)S(1)}) custom-call(s32[1]{0:T(128)S(6)} %copy.11.counts_hbm, s32[1,6]{1,0:T(1,128)} %chosen_hbm.1, s32[1,8]{1,0:T(1,128)} %row_hbm.1, s32[1,8]{1,0:T(1,128)} %column_hbm.1, f32[2,8,256,256]{3,2,1,0:T(8,128)} %bitcast.4, ...), custom_call_target="tpu_custom_call" | custom-call | tf_op jit(solution)/shard_map/slots/pallas_call | solution.py:570
  48.9 2.2 %deposit.1 = f32[2,8,256,256]{3,2,1,0:T(8,128)} custom-call(f32[3,8,128]{2,1,0:T(8,128)S(1)} %get-tuple-element.8.index_in, f32[8,2,256,256]{3,2,1,0:T(8,128)S(1)} %get-tuple-element.9.canvas, bf16[2,256,256]{2,1,0:T(8,128)(2,1)S(1)} %get-tuple-element.10.final), custom_call_target="tpu_custom_call" | custom-call | tf_op jit(solution)/shard_map/deposit/pallas_call | solution.py:629
